TPU v7x, 256 devices: a whole 4x4x8 slice. The times are simulated.
256 devices in a mesh: expert: 32 (over y, z), unit: 8 (over x, core).
Axes of the slice: x: 4, y: 4, z: 8, core: 2. Of those that a mesh axis runs over, the one named last changes fastest.
Arguments:
- w_up: bfloat16 [128, 1536, 4096], P('expert', 'unit'), may hold values from -0.09375 to 0.09375
- cluster: int32 [128, 1], replicated, may hold values from 0 to 31
- counts: int32 [128], replicated, may hold values from 16 to 127
Outputs:
- merged: bfloat16 [32, 1536, 4096], P('expert', None, 'unit')
Inputs may be any that keep to these rules, and one draw needn't show every extreme that they name: Every cluster has at least one member.
All inputs are finite; a program needn't handle non-finite values.
Results may differ from a plain program's by a relative error of at most 0.0051.
Values may be sent and summed in bfloat16 or wider, within the bound.
No kernel may reach another device: no remote copies, remote signals or barrier semaphores. Data moves between devices by JAX's collectives and lax.ppermute only.
A program may use at most 128 MiB of HBM per device.

v0:
```python
import jax
import jax.numpy as jnp
from jax import lax
from jax.sharding import PartitionSpec as P

BLOCK = 96
NS_STEPS = 8
CLU_DEV = 1


def newton_schulz(matrices):
    frob_norm = jnp.sqrt(jnp.sum(matrices * matrices, axis=(-2, -1), keepdims=True) + 1e-06)
    value = matrices / frob_norm
    for iteration in range(NS_STEPS):
        square = jnp.einsum("...ij,...kj->...ik", value, value, precision=lax.Precision.HIGHEST)
        value = 1.5 * value - 0.5 * jnp.einsum(
            "...ik,...kj->...ij", square, value, precision=lax.Precision.HIGHEST
        )
    return value


def block_gram(left, right):
    experts, units, width = left.shape
    nblocks = units // BLOCK
    lead_rows = left.reshape(experts, nblocks, BLOCK, width)
    member_rows = right.reshape(experts, nblocks, BLOCK, width)
    gram = jnp.einsum("nbid,nbjd->nibj", lead_rows, member_rows, preferred_element_type=jnp.float32)
    return gram.reshape(experts, BLOCK, units)


def polar_factors(gram):
    experts, height, units = gram.shape
    nblocks = units // BLOCK
    matrices = gram.reshape(experts, BLOCK, nblocks, BLOCK).transpose(0, 2, 1, 3)
    polar = newton_schulz(matrices).astype(jnp.bfloat16)
    return polar.transpose(0, 2, 1, 3).reshape(experts, BLOCK, units)


def align_rows(factors, slab, scale):
    experts, units, width = slab.shape
    nblocks = units // BLOCK
    turn = factors.reshape(experts, BLOCK, nblocks, BLOCK)
    member_rows = slab.reshape(experts, nblocks, BLOCK, width)
    turned = jnp.einsum("nibj,nbjd->nbid", turn, member_rows, preferred_element_type=jnp.float32)
    turned = turned * scale[:, None, None, None]
    return turned.reshape(experts, units, width).astype(jnp.bfloat16)


def on_device(w_up, cluster, counts):
    cluster_ids = cluster[:, 0]
    experts = cluster_ids.shape[0]
    clusters = CLU_DEV * lax.axis_size("expert")
    index = jnp.arange(experts, dtype=jnp.int32)
    labels = jnp.arange(clusters, dtype=jnp.int32)
    member = cluster_ids[None, :] == labels[:, None]
    score = counts * experts + (experts - 1 - index)
    best = jnp.max(jnp.where(member, score[None, :], -1), axis=1)
    leader = experts - 1 - best % experts
    anchor_of = jnp.sum(jnp.where(member, leader[:, None], 0), axis=0)
    total = jnp.sum(jnp.where(member, counts[None, :], 0), axis=1).astype(jnp.float32)
    weight = counts.astype(jnp.float32) / jnp.sum(jnp.where(member, total[:, None], 0.0), axis=0)
    columns = lax.all_to_all(w_up, "expert", split_axis=2, concat_axis=0, tiled=True)
    anchors = jnp.take(columns, anchor_of, axis=0)
    gram = lax.psum_scatter(block_gram(anchors, columns), "expert", scatter_dimension=0, tiled=True)
    polar = polar_factors(gram)
    aligned = align_rows(lax.all_gather(polar, "expert", axis=0, tiled=True), columns, weight)
    select = member.astype(jnp.bfloat16)
    summed = jnp.dot(select, aligned.reshape(experts, -1), preferred_element_type=jnp.float32)
    merged = summed.reshape(clusters, aligned.shape[1], aligned.shape[2]).astype(jnp.bfloat16)
    return lax.all_to_all(
        lax.all_to_all(merged, "expert", split_axis=0, concat_axis=2, tiled=True),
        "unit",
        split_axis=2,
        concat_axis=1,
        tiled=True,
    )


def solution(mesh):
    return jax.shard_map(
        on_device,
        mesh=mesh,
        in_specs=(P("expert", "unit", None), P(), P()),
        out_specs=P("expert", None, "unit"),
        check_vma=False,
    )
```

profile of v0, /device:TPU:1, one launch (start us, length us, event | category | flops | bytes accessed | tf_op | source)
XLA Modules:
  0.0 799.8 jit_solution(10294570698834870266)
XLA Ops:
  6.5 13.1 %copy.44 = bf16[4,192,4096]{1,0,2:T(4,128)(2,1)} copy(bf16[4,192,4096]{2,1,0:T(8,128)(2,1)} %param.3) | data formatting | bytes 12582912 | tf_op args[0]
  19.6 12.3 %all-to-all-start = ((bf16[4,192,4096]{1,0,2:T(4,128)(2,1)}), bf16[4,192,4096]{1,0,2:T(4,128)(2,1)}, u32[]{:S(2)}, u32[]{:S(2)}) async-start(bf16[4,192,4096]{1,0,2:T(4,128)(2,1)} %copy.44), calls=%async_computation | async-start | bytes 16777216 | tf_op jit(solution)/shard_map/all_to_all | solution.py:62
  32.3 187.8 %all-to-all-done = bf16[4,192,4096]{1,0,2:T(4,128)(2,1)} async-done(((bf16[4,192,4096]{1,0,2:T(4,128)(2,1)}), bf16[4,192,4096]{1,0,2:T(4,128)(2,1)}, u32[]{:S(2)}, u32[]{:S(2)}) %all-to-all-start) | async-done | bytes 6291488 | tf_op jit(solution)/shard_map/all_to_all | solution.py:62
  220.1 13.2 %copy.45 = bf16[4,192,32,128]{3,1,0,2:T(8,128)(2,1)} copy(bf16[4,192,32,128]{1,0,3,2:T(4,128)(2,1)} %bitcast.2) | data formatting | bytes 12582912 | tf_op jit(solution)/shard_map/all_to_all | solution.py:62
  233.3 6.7 gather_fusion
  240.0 13.4 %fusion.3 = f32[128,96,2,96]{3,1,2,0:T(8,128)} fusion(bf16[128,2,96,128]{3,2,1,0:T(8,128)(2,1)} %bitcast.128, bf16[128,2,96,128]{3,2,1,0:T(8,128)(2,1)} %bitcast.134, pred[128]{0:T(512)(128)(4,1)S(1)} %compare_and_fusion), kind=kOutput, calls=%fused_computation.6 | convolution fusion | flops 607125504 | bytes 22020224 | tf_op jit(solution)/shard_map/nbid,nbjd->nibj/dot_general | solution.py:27
  253.5 11.7 %copy.46 = f32[128,96,2,96]{0,3,2,1:T(8,128)} copy(f32[128,96,2,96]{3,1,2,0:T(8,128)} %fusion.3) | data formatting | bytes 18874368 | tf_op jit(solution)/shard_map/nbid,nbjd->nibj/transpose | solution.py:27
  265.2 12.7 %copy.47 = f32[128,96,192]{2,1,0:T(8,128)} copy(f32[128,96,192]{0,2,1:T(8,128)} %bitcast.130) | data formatting | bytes 18874368 | tf_op jit(solution)/shard_map/reshape | solution.py:28
  278.1 237.5 %reduce-scatter.2.cloned.1.call-done = f32[4,96,192]{2,1,0:T(8,128)} async-done(((f32[128,96,192]{2,1,0:T(8,128)}), f32[4,96,192]{2,1,0:T(8,128)}) %reduce-scatter.2.cloned.1.call-update) | async-done | bytes 294928 | tf_op jit(solution)/shard_map/reduce_scatter | solution.py:64
  530.4 90.1 %all-gather.2.cloned.1.call-done = bf16[128,96,192]{2,1,0:T(8,128)(2,1)} async-done(((bf16[4,96,192]{2,1,0:T(8,128)(2,1)}), bf16[128,96,192]{2,1,0:T(8,128)(2,1)}) %all-gather.2.cloned.1.call-update) | async-done | bytes 4718608 | tf_op jit(solution)/shard_map/all_gather | solution.py:66
  620.5 8.8 %copy.52 = bf16[128,96,192]{0,2,1:T(8,128)(2,1)} copy(bf16[128,96,192]{2,1,0:T(8,128)(2,1)} %all-gather.2.cloned.1.call-done) | data formatting | bytes 9437184 | tf_op jit(solution)/shard_map/all_gather | solution.py:66
  629.2 8.5 %copy.53 = bf16[128,96,2,96]{3,1,2,0:T(8,128)(2,1)} copy(bf16[128,96,2,96]{0,3,2,1:T(8,128)(2,1)} %bitcast.135) | data formatting | bytes 9437184 | tf_op jit(solution)/shard_map/reshape | solution.py:42
  637.7 6.4 multiply_convert_fusion
  644.1 8.0 %copy.65 = bf16[16,8,192,128]{3,1,2,0:T(8,128)(2,1)} copy(bf16[16,8,192,128]{3,2,1,0:T(8,128)(2,1)S(1)} %bitcast.133) | data formatting | bytes 12582912
  652.2 8.6 %copy.54 = bf16[24576,128]{1,0:T(8,128)(2,1)} copy(bf16[24576,128]{0,1:T(8,128)(2,1)} %bitcast.131) | data formatting | bytes 12582912 | tf_op jit(solution)/shard_map/dot_general | solution.py:68
  660.8 4.9 convolution_convert_fusion
  666.4 41.9 %all_to_all.54 = bf16[32,192,128]{2,1,0:T(8,128)(2,1)} all-to-all(bf16[32,192,128]{2,1,0:T(8,128)(2,1)S(1)} %copy.55), channel_id=1, replica_groups=mesh['expert'=32,'unit'=8] {'expert'}, dimensions={0} | all-to-all | bytes 3145728 | tf_op jit(solution)/shard_map/all_to_all | solution.py:71
  708.3 3.1 copy.60
  711.4 6.2 reshape.84
  718.1 23.6 %reduce.1 = bf16[4096,192]{1,0:T(8,128)(2,1)S(1)} reduce(bf16[4096,1,192]{2,1,0:T(2,128)(2,1)} %bitcast.136, bf16[]{:T(256)} %broadcast.142), dimensions={1}, to_apply=%bitcast.99.reduce_sub_computation | reduce | bytes 3145730
  741.8 4.4 reshape.85
  746.1 29.5 %all_to_all.55 = bf16[8,2,49152]{2,1,0:T(2,128)(2,1)S(1)} all-to-all(bf16[8,2,49152]{2,1,0:T(2,128)(2,1)} %reshape.85), channel_id=1, replica_groups=mesh['expert'=32,'unit'=8] {'unit'}, dimensions={0} | all-to-all | bytes 3145728 | tf_op jit(solution)/shard_map/all_to_all | solution.py:70
  775.7 4.9 reshape.86
  780.6 9.9 %copy.58 = bf16[1,192,4096]{2,1,0:T(8,128)(2,1)S(1)} copy(bf16[1,192,4096]{1,0,2:T(2,128)(2,1)} %bitcast.137) | data formatting | bytes 3145728 | tf_op jit(solution)/shard_map/all_to_all | solution.py:70
  (45 shorter events, 18.7 us)
Async XLA Ops:
  19.6 12.3 %copy-start.1 = (s32[128]{0:T(128)S(1)}, s32[128]{0:T(128)}, u32[]{:S(2)}) copy-start(s32[128]{0:T(128)} %param.5) | copy-start | bytes 1540
  19.6 12.4 %copy-start = (s32[128,1]{0,1:T(1,128)S(1)}, s32[128,1]{0,1:T(1,128)}, u32[]{:S(2)}) copy-start(s32[128,1]{0,1:T(1,128)} %param.4) | copy-start | bytes 1540
  19.6 200.5 %all-to-all-start = ((bf16[4,192,4096]{1,0,2:T(4,128)(2,1)}), bf16[4,192,4096]{1,0,2:T(4,128)(2,1)}, u32[]{:S(2)}, u32[]{:S(2)}) async-start(bf16[4,192,4096]{1,0,2:T(4,128)(2,1)} %copy.44), calls=%async_computation | async-start | bytes 16777216 | tf_op jit(solution)/shard_map/all_to_all | solution.py:62
  31.9 483.7 %reduce-scatter.2.cloned.1.call-start = ((), (), s32[]{:S(2)}) async-start(), calls=%async_computation.4 | async-start | bytes 12976128 | tf_op jit(solution)/shard_map/reduce_scatter | solution.py:64
  277.9 342.6 %all-gather.2.cloned.1.call-start = ((), (), s32[]{:S(2)}) async-start(), calls=%async_computation.5 | async-start | bytes 6488064 | tf_op jit(solution)/shard_map/all_gather | solution.py:66
Sparse Core Ops, SparseCore 0:
  278.0 237.5 reduce-scatter.1
  530.4 90.0 all-gather.1
where the time goes:
time: 802 us; the launch traced here: 800 us
  waiting for transfers between devices  515 us (64%)
  local copies, waits for them, and re-layouts  126 us (16%)
  blocking collectives  71.4 us (9%)
  matrix products  36.8 us (5%)
  other arithmetic  24.2 us (3%)
  between operations  13.7 us (2%)
  starting transfers between devices  12.5 us (2%)
    reduce_scatter x1, waiting for transfers between devices, on_device(): lax.psum_scatter(block_gram(anchors, columns), 'expert', scatter_dimensio...  237 us
    all_to_all x1, waiting for transfers between devices, on_device(): lax.all_to_all(w_up, 'expert', split_axis=2, concat_axis=0, tiled=True)  188 us
    all_gather x1, waiting for transfers between devices, on_device(): lax.all_gather(polar, 'expert', axis=0, tiled=True)  90.1 us
    all_to_all x1, blocking collectives, on_device(): lax.all_to_all(merged, 'expert', split_axis=0, concat_axis=2, tiled=True)  41.9 us
    unnamed x10, local copies, waits for them, and re-layouts  31.6 us
    all_to_all x1, blocking collectives, on_device(): lax.all_to_all(lax.all_to_all(merged, 'expert', split_axis=0, concat_axis...  29.5 us
    unnamed x1, other arithmetic  23.6 us
  transfers between devices with their start and end apart: 3, of which 3 were waited for; matrix products, arithmetic and copies ran while one was open for 0% of the time, Pallas kernels for 0%

commit v1 on v0

v1 whole, which is shorter than its diff:
```python
import jax
import jax.numpy as jnp
from jax import lax
from jax.experimental import pallas as pl
from jax.experimental.pallas import tpu as pltpu
from jax.sharding import Mesh, PartitionSpec as P

BLOCK = 96
NS_STEPS = 8
NY, NZ, NX, NC = 4, 8, 4, 2
EXPERTS = 128
CLUSTERS = 32
COLS = 256
VMEM = pl.BlockSpec(memory_space=pltpu.VMEM)
SMEM = pl.BlockSpec(memory_space=pltpu.SMEM)


def newton_schulz(matrices):
    frob_norm = jnp.sqrt(jnp.sum(matrices * matrices, axis=(-2, -1), keepdims=True) + 1e-06)
    value = matrices / frob_norm
    for iteration in range(NS_STEPS):
        square = jnp.einsum("...ij,...kj->...ik", value, value, precision=lax.Precision.HIGHEST)
        value = 1.5 * value - 0.5 * jnp.einsum(
            "...ik,...kj->...ij", square, value, precision=lax.Precision.HIGHEST
        )
    return value


def spread_kernel(w_ref, o_ref):
    for s in range(NZ * NC):
        o_ref[s % NC, 0, s // NC, 0] = w_ref[0, :, s * COLS:(s + 1) * COLS]


def spread(w):
    experts, units, width = w.shape
    return pl.pallas_call(
        spread_kernel,
        grid=(experts, units // BLOCK),
        in_specs=[pl.BlockSpec((1, BLOCK, width), lambda e, j: (e, j, 0))],
        out_specs=pl.BlockSpec((NC, 1, NZ, 1, BLOCK, COLS), lambda e, j: (0, j, 0, e, 0, 0)),
        out_shape=jax.ShapeDtypeStruct((NC, units // BLOCK, NZ, experts, BLOCK, COLS), w.dtype),
    )(w)


def gram_kernel(anchor_ref, core_ref, w_ref, keep_ref, send_ref):
    half = EXPERTS // NC
    core = core_ref[0]

    def one(m):
        return lax.dot_general(
            w_ref[anchor_ref[m]], w_ref[m], (((1,), (1,)), ((), ())), preferred_element_type=jnp.float32
        )

    def step(i, carry):
        keep_ref[i] = one(core * half + i)
        send_ref[i] = one((1 - core) * half + i)
        return carry

    lax.fori_loop(0, half, step, 0, unroll=4)


def grams(anchor_of, core, columns):
    shape = jax.ShapeDtypeStruct((EXPERTS // NC, BLOCK, BLOCK), jnp.float32)
    return pl.pallas_call(
        gram_kernel, in_specs=[SMEM, SMEM, VMEM], out_specs=[VMEM, VMEM], out_shape=[shape, shape]
    )(anchor_of, core, columns)


def align_kernel(slot_ref, weight_ref, polar_ref, w_ref, o_ref, acc_ref):
    acc_ref[...] = jnp.zeros_like(acc_ref)
    half = EXPERTS // NC

    def step(m, carry):
        place = ((m % half) // 8 * NC + m // half) * 8 + m % 8
        turned = jnp.dot(polar_ref[place], w_ref[m], preferred_element_type=jnp.float32)
        turned = (turned * weight_ref[m]).astype(jnp.bfloat16).astype(jnp.float32)
        slot = slot_ref[m]
        acc_ref[slot] = acc_ref[slot] + turned
        return carry

    lax.fori_loop(0, EXPERTS, step, 0, unroll=4)
    o_ref[...] = acc_ref[...].astype(o_ref.dtype)


def align(slot_of, weight, polar, columns):
    return pl.pallas_call(
        align_kernel,
        in_specs=[SMEM, SMEM, VMEM, VMEM],
        out_specs=VMEM,
        out_shape=jax.ShapeDtypeStruct((CLUSTERS, BLOCK, COLS), jnp.bfloat16),
        scratch_shapes=[pltpu.VMEM((CLUSTERS, BLOCK, COLS), jnp.float32)],
    )(slot_of, weight, polar, columns)


def on_device(w_up, cluster, counts):
    cluster_ids = cluster[:, 0]
    index = jnp.arange(EXPERTS, dtype=jnp.int32)
    labels = jnp.arange(CLUSTERS, dtype=jnp.int32)
    member = cluster_ids[None, :] == labels[:, None]
    score = counts * EXPERTS + (EXPERTS - 1 - index)
    best = jnp.max(jnp.where(member, score[None, :], -1), axis=1)
    leader = EXPERTS - 1 - best % EXPERTS
    anchor_of = jnp.sum(jnp.where(member, leader[:, None], 0), axis=0)
    total = jnp.sum(jnp.where(member, counts[None, :], 0), axis=1).astype(jnp.float32)
    weight = counts.astype(jnp.float32) / jnp.sum(jnp.where(member, total[:, None], 0.0), axis=0)
    slot_of = cluster_ids % NZ * NY + cluster_ids // NZ
    core = lax.axis_index("core").astype(jnp.int32).reshape(1)

    rows = spread(w_up)
    rows = lax.all_to_all(rows, "core", split_axis=0, concat_axis=0, tiled=True)
    rows = rows.reshape(NY * NZ, 4 * BLOCK, COLS)
    columns = lax.all_to_all(rows, ("y", "z"), split_axis=0, concat_axis=0, tiled=True)
    columns = columns.reshape(EXPERTS, BLOCK, COLS)

    keep, send = grams(anchor_of, core, columns)
    partial = keep + lax.ppermute(send, "core", [(0, 1), (1, 0)])
    gram = lax.psum_scatter(partial, "z", scatter_dimension=0, tiled=True)
    polar = newton_schulz(gram).astype(jnp.bfloat16)
    polar = lax.all_gather(polar, ("z", "core"), axis=0, tiled=True)
    merged = align(slot_of, weight, polar, columns)

    merged = lax.all_to_all(merged, ("z", "y"), split_axis=0, concat_axis=0, tiled=True)
    merged = merged.reshape(NZ, NY * BLOCK, COLS)
    merged = lax.all_to_all(merged, ("x", "core"), split_axis=0, concat_axis=0, tiled=True)
    merged = merged.reshape(NX, NC, NY * BLOCK, COLS).transpose(0, 2, 1, 3)
    return merged.reshape(1, NX * NY * BLOCK, NC * COLS)


def solution(mesh):
    grid = Mesh(mesh.devices.reshape(NY, NZ, NX, NC), ("y", "z", "x", "core"))
    return jax.shard_map(
        on_device,
        mesh=grid,
        in_specs=(P(("y", "z"), ("x", "core"), None), P(), P()),
        out_specs=P(("y", "z"), None, ("x", "core")),
        check_vma=False,
    )
```

time: 802 us -> 402 us (0.50)
  waiting for transfers between devices: 515 us -> 231 us
  local copies, waits for them, and re-layouts: 126 us -> 3.89 us
  Pallas kernels: 0 us -> 29.3 us
  matrix products: 36.8 us -> 14.5 us
  blocking collectives: 71.4 us -> 90.9 us
  other arithmetic: 24.2 us -> 7.24 us
    reduce_scatter x1, waiting for transfers between devices: 237 us -> 43.9 us  [on_device(): gram = lax.psum_scatter(partial, 'z', scatter_dimension=0, tiled=True)]
    all_to_all x1, waiting for transfers between devices: 188 us -> 139 us  [on_device(): lax.all_to_all(rows, ('y', 'z'), split_axis=0, concat_axis=0, tiled=True)]
    all_gather x1, waiting for transfers between devices: 90.1 us -> 42.3 us  [on_device(): polar = lax.all_gather(polar, ('z', 'core'), axis=0, tiled=True)]
    all_to_all x6 -> x0, local copies, waits for them, and re-layouts: 34.1 us -> none  [the longest x1 13.2 us: on_device(): lax.all_to_all(w_up, 'expert', split_axis=2, concat_axis=0, tiled=True)]
    unnamed x10 -> x4, local copies, waits for them, and re-layouts: 31.6 us -> 0.01 us
    pallas_call x0 -> x3, Pallas kernels: none -> 29.3 us  [the longest x1 11.9 us: align(): pl.pallas_call(align_kernel, in_specs=[SMEM, SMEM, VMEM, VMEM], out_specs...]
    dot_general x3 -> x0, matrix products: 24.8 us -> none  [the longest x1 13.4 us: block_gram(): jnp.einsum('nbid,nbjd->nibj', lead_rows, member_rows, preferred_element_t...]
    unnamed x1 -> x0, other arithmetic: 23.6 us -> none
  transfers between devices with their start and end apart: 3 -> 4, of which waited for: 3 -> 4; matrix products, arithmetic and copies ran while one was open for 0% -> 0% of each run, Pallas kernels for 0% -> 0%
where the time goes in v1:
time: 402 us; the launch traced here: 401 us
  waiting for transfers between devices  231 us (57%)
  blocking collectives  90.9 us (23%)
  Pallas kernels  29.3 us (7%)
  matrix products  14.5 us (4%)
  between operations  13.6 us (3%)
  starting transfers between devices  11.2 us (3%)
  other arithmetic  7.24 us (2%)
    all_to_all x1, waiting for transfers between devices, on_device(): lax.all_to_all(rows, ('y', 'z'), split_axis=0, concat_axis=0, tiled=True)  139 us
    all_to_all x1, blocking collectives, on_device(): lax.all_to_all(merged, ('z', 'y'), split_axis=0, concat_axis=0, tiled=True)  46.2 us
    reduce_scatter x1, waiting for transfers between devices, on_device(): gram = lax.psum_scatter(partial, 'z', scatter_dimension=0, tiled=True)  43.9 us
    all_gather x1, waiting for transfers between devices, on_device(): polar = lax.all_gather(polar, ('z', 'core'), axis=0, tiled=True)  42.3 us
    all_to_all x1, blocking collectives, on_device(): lax.all_to_all(merged, ('x', 'core'), split_axis=0, concat_axis=0, tiled=...  26.6 us
    all_to_all x1, blocking collectives, on_device(): rows = lax.all_to_all(rows, 'core', split_axis=0, concat_axis=0, tiled=True)  18.1 us
    pallas_call x1, Pallas kernels, align(): pl.pallas_call(align_kernel, in_specs=[SMEM, SMEM, VMEM, VMEM], out_specs...  11.9 us
    all_to_all x1, starting transfers between devices, on_device(): lax.all_to_all(rows, ('y', 'z'), split_axis=0, concat_axis=0, tiled=True)  9.74 us
  transfers between devices with their start and end apart: 4, of which 4 were waited for; matrix products, arithmetic and copies ran while one was open for 0% of the time, Pallas kernels for 0%

profile of v1, /device:TPU:1, one launch (start us, length us, event | category | flops | bytes accessed | tf_op | source)
XLA Modules:
  0.0 401.3 jit_solution(16092902133721102288)
XLA Ops:
  6.5 7.9 %shard_map.37 = bf16[2,2,8,4,96,256]{5,4,3,2,1,0:T(8,128)(2,1)} custom-call(bf16[4,192,4096]{2,1,0:T(8,128)(2,1)} %w_ref.1), custom_call_target="tpu_custom_call" | custom-call | tf_op jit(solution)/shard_map/pallas_call | solution.py:36
  14.4 18.1 %all_to_all.20 = bf16[2,2,8,4,96,256]{5,4,3,2,1,0:T(8,128)(2,1)} all-to-all(bf16[2,2,8,4,96,256]{5,4,3,2,1,0:T(8,128)(2,1)} %shard_map.37), channel_id=1, replica_groups=mesh['y'=4,'z'=8,'x'=4,'core'=2] {'core'}, dimensions={0} | all-to-all | bytes 12582912 | tf_op jit(solution)/shard_map/all_to_all | solution.py:110
  32.5 9.7 %all-to-all-start.1 = ((bf16[32,384,256]{2,1,0:T(8,128)(2,1)}), bf16[32,384,256]{2,1,0:T(8,128)(2,1)}, u32[]{:S(2)}, u32[]{:S(2)}) async-start(bf16[32,384,256]{2,1,0:T(8,128)(2,1)} %bitcast.39), calls=%async_computation.1 | async-start | bytes 12582912 | tf_op jit(solution)/shard_map/all_to_all | solution.py:112
  43.1 138.9 %all-to-all-done.1 = bf16[32,384,256]{2,1,0:T(8,128)(2,1)} async-done(((bf16[32,384,256]{2,1,0:T(8,128)(2,1)}), bf16[32,384,256]{2,1,0:T(8,128)(2,1)}, u32[]{:S(2)}, u32[]{:S(2)}) %all-to-all-start.1) | async-done | bytes 6291488 | tf_op jit(solution)/shard_map/all_to_all | solution.py:112
  182.0 9.6 %shard_map.38 = (f32[64,96,96]{2,1,0:T(8,128)}, f32[64,96,96]{2,1,0:T(8,128)}) custom-call(s32[128]{0:T(128)} %get-tuple-element.9.anchor_ref, s32[1]{0:T(128)} %bitcast.1.core_ref, bf16[128,96,256]{2,1,0:T(8,128)(2,1)} %bitcast.3.w_ref), custom_call_target="tpu_custom_call" | custom-call | tf_op jit(solution)/shard_map/pallas_call | solution.py:64
  191.6 1.4 collective-permute-start
  193.0 5.5 %collective-permute-done = f32[64,96,96]{2,1,0:T(8,128)S(1)} collective-permute-done((f32[64,96,96]{2,1,0:T(8,128)}, f32[64,96,96]{2,1,0:T(8,128)S(1)}, u32[]{:S(2)}, u32[]{:S(2)}) %collective-permute-start) | collective-permute-done | bytes 2359328 | tf_op jit(solution)/shard_map/ppermute | solution.py:116
  198.5 4.1 %add.40 = f32[64,96,96]{2,1,0:T(8,128)} add(f32[64,96,96]{2,1,0:T(8,128)} %get-tuple-element.7, f32[64,96,96]{2,1,0:T(8,128)S(1)} %collective-permute-done) | non-fusion elementwise | flops 589824 | bytes 7077888 | tf_op jit(solution)/shard_map/add | solution.py:116
  202.6 43.9 %reduce-scatter.2.cloned.1.call-done = f32[8,96,96]{2,1,0:T(8,128)} async-done(((f32[64,96,96]{2,1,0:T(8,128)}), f32[8,96,96]{2,1,0:T(8,128)}) %reduce-scatter.2.cloned.1.call-update) | async-done | bytes 294928 | tf_op jit(solution)/shard_map/reduce_scatter | solution.py:117
  246.5 1.2 multiply_reduce_fusion
  247.7 2.1 fusion.8
  249.8 1.7 multiply_subtract_fusion
  251.5 0.9 fusion.13
  253.0 0.9 fusion.14
  254.4 0.9 fusion.15
  255.9 0.9 fusion.16
  257.3 0.9 fusion.17
  261.1 1.2 fusion.7
  263.6 42.3 %all-gather.2.cloned.1.call-done.polar_ref = bf16[128,96,96]{2,1,0:T(8,128)(2,1)} async-done(((bf16[8,96,96]{2,1,0:T(8,128)(2,1)}), bf16[128,96,96]{2,1,0:T(8,128)(2,1)}) %all-gather.2.cloned.1.call-update) | async-done | bytes 2359312 | tf_op jit(solution)/shard_map/all_gather | solution.py:119
  305.9 11.9 %shard_map.39 = bf16[32,96,256]{2,1,0:T(8,128)(2,1)} custom-call(s32[128]{0:T(128)} %fusion.10.slot_ref, f32[128]{0:T(128)} %convert_divide_fusion.weight_ref, bf16[128,96,96]{2,1,0:T(8,128)(2,1)} %all-gather.2.cloned.1.call-done.polar_ref, bf16[128,96,256]{2,1,0:T(8,128)(2,1)} %bitcast.3.w_ref), custom_call_target="tpu_custom_call" | custom-call | tf_op jit(solution)/shard_map/pallas_call | solution.py:86
  317.8 46.2 %all_to_all.21 = bf16[32,96,256]{2,1,0:T(8,128)(2,1)S(1)} all-to-all(bf16[32,96,256]{2,1,0:T(8,128)(2,1)} %shard_map.39), channel_id=1, replica_groups=mesh['y'=4,'z'=8,'x'=4,'core'=2] {'z','y'}, dimensions={0} | all-to-all | bytes 3145728 | tf_op jit(solution)/shard_map/all_to_all | solution.py:122
  364.0 26.6 %all_to_all.22 = bf16[8,384,256]{2,1,0:T(8,128)(2,1)S(1)} all-to-all(bf16[8,384,256]{2,1,0:T(8,128)(2,1)S(1)} %bitcast.40), channel_id=1, replica_groups=mesh['y'=4,'z'=8,'x'=4,'core'=2] {'x','core'}, dimensions={0} | all-to-all | bytes 3145728 | tf_op jit(solution)/shard_map/all_to_all | solution.py:124
  390.6 1.6 copy.8
  392.2 2.3 reshape.49
  (25 shorter events, 7.2 us)
Async XLA Ops:
  32.5 9.8 %copy-start.1 = (s32[128]{0:T(128)S(1)}, s32[128]{0:T(128)}, u32[]{:S(2)}) copy-start(s32[128]{0:T(128)} %param.5) | copy-start | bytes 1540
  32.5 9.8 %copy-start = (s32[128,1]{0,1:T(1,128)S(1)}, s32[128,1]{0,1:T(1,128)}, u32[]{:S(2)}) copy-start(s32[128,1]{0,1:T(1,128)} %param.4) | copy-start | bytes 1540
  32.5 149.5 %all-to-all-start.1 = ((bf16[32,384,256]{2,1,0:T(8,128)(2,1)}), bf16[32,384,256]{2,1,0:T(8,128)(2,1)}, u32[]{:S(2)}, u32[]{:S(2)}) async-start(bf16[32,384,256]{2,1,0:T(8,128)(2,1)} %bitcast.39), calls=%async_computation.1 | async-start | bytes 12582912 | tf_op jit(solution)/shard_map/all_to_all | solution.py:112
  42.3 204.3 %reduce-scatter.2.cloned.1.call-start = ((), (), s32[]{:S(2)}) async-start(), calls=%async_computation.5 | async-start | bytes 3538944 | tf_op jit(solution)/shard_map/reduce_scatter | solution.py:117
  191.6 6.9 %collective-permute-start = (f32[64,96,96]{2,1,0:T(8,128)}, f32[64,96,96]{2,1,0:T(8,128)S(1)}, u32[]{:S(2)}, u32[]{:S(2)}) collective-permute-start(f32[64,96,96]{2,1,0:T(8,128)} %get-tuple-element.8), channel_id=1, source_target_pairs={{0,1},{1,0},{2,3},{3,2},{4,5},{5,4},{6,7},{7,6},{8,9},{9,8},{10,11... | collective-permute-start | bytes 7077896 | tf_op jit(solution)/shard_map/ppermute | solution.py:116
  202.6 103.3 %all-gather.2.cloned.1.call-start = ((), (), s32[]{:S(2)}) async-start(), calls=%async_computation.6 | async-start | bytes 3342336 | tf_op jit(solution)/shard_map/all_gather | solution.py:119
Sparse Core Ops, SparseCore 0:
  202.7 43.8 reduce-scatter.1
  262.4 43.4 all-gather.1

commit v2 on v1

v2 whole, which is shorter than its diff:
```python
import jax
import jax.numpy as jnp
from jax import lax
from jax.experimental import pallas as pl
from jax.experimental.pallas import tpu as pltpu
from jax.sharding import Mesh, PartitionSpec as P

BLOCK = 96
NS_STEPS = 8
NY, NZB, NZC, NX, NC = 4, 4, 2, 4, 2
EXPERTS = 128
CLUSTERS = 32
COLS = 256
PACK = 4
LANES = PACK * BLOCK
SLICES = NY * NZC
GROUPS = EXPERTS // PACK // NC
MINE = GROUPS // SLICES
SWAP = [(0, 1), (1, 0)]
VMEM = pl.BlockSpec(memory_space=pltpu.VMEM)
SMEM = pl.BlockSpec(memory_space=pltpu.SMEM)


def flip(position):
    return ((position >> 3) & 3) * 32 + (position >> 5) * 8 + (position & 7)


def spread_kernel(core_ref, w_ref, o_ref, *, other):
    half = 1 - core_ref[0] if other else core_ref[0]
    for u in range(SLICES):
        start = pl.multiple_of((2 * u + half) * COLS, COLS)
        o_ref[0, u, 0] = w_ref[0, :, pl.ds(start, COLS)]


def spread(core, w, other):
    experts, units, width = w.shape
    blocks = units // BLOCK

    def kernel(core_ref, w_ref, o_ref):
        spread_kernel(core_ref, w_ref, o_ref, other=other)

    def place(e, j, core_ref):
        return (j if other else core_ref[0] * blocks + j, 0, e, 0, 0)

    return pl.pallas_call(
        kernel,
        grid_spec=pltpu.PrefetchScalarGridSpec(
            num_scalar_prefetch=1,
            grid=(experts, blocks),
            in_specs=[pl.BlockSpec((1, BLOCK, width), lambda e, j, core_ref: (e, j, 0))],
            out_specs=pl.BlockSpec((1, SLICES, 1, BLOCK, COLS), place),
        ),
        out_shape=jax.ShapeDtypeStruct((blocks if other else NC * blocks, SLICES, experts, BLOCK, COLS), w.dtype),
    )(core, w)


def join_kernel(core_ref, got_ref, held_ref, o_ref):
    o_ref[...] = got_ref[...]


def join(core, got, held):
    blocks, slices, experts, _, _ = got.shape
    block = (1, 2, experts, BLOCK, COLS)
    return pl.pallas_call(
        join_kernel,
        grid_spec=pltpu.PrefetchScalarGridSpec(
            num_scalar_prefetch=1,
            grid=(blocks, slices // 2),
            in_specs=[
                pl.BlockSpec(block, lambda j, u, core_ref: (j, u, 0, 0, 0)),
                pl.BlockSpec(memory_space=pl.ANY),
            ],
            out_specs=pl.BlockSpec(block, lambda j, u, core_ref: ((1 - core_ref[0]) * blocks + j, u, 0, 0, 0)),
        ),
        out_shape=jax.ShapeDtypeStruct(held.shape, held.dtype),
        input_output_aliases={2: 0},
    )(core, got, held)


def grams(anchor_of, core, columns, other):
    def kernel(anchor_ref, core_ref, w_ref, o_ref):
        half = 1 - core_ref[0] if other else core_ref[0]

        def step(g, carry):
            parts = []
            for i in range(PACK):
                p = (half * GROUPS + g) * PACK + i
                lead = flip(anchor_ref[flip(p)])
                parts.append(
                    lax.dot_general(
                        w_ref[lead], w_ref[p], (((1,), (1,)), ((), ())), preferred_element_type=jnp.float32
                    )
                )
            o_ref[g] = jnp.concatenate(parts, axis=1)
            return carry

        lax.fori_loop(0, GROUPS, step, 0)

    return pl.pallas_call(
        kernel,
        in_specs=[SMEM, SMEM, VMEM],
        out_specs=VMEM,
        out_shape=jax.ShapeDtypeStruct((GROUPS, BLOCK, LANES), jnp.float32),
    )(anchor_of, core, columns)


def polar_kernel(part_ref, o_ref, x_ref):
    count = MINE * PACK
    for g in range(MINE):
        total = part_ref[0, g]
        for s in range(1, SLICES):
            total = total + part_ref[s, g]
        for i in range(PACK):
            gram = total[:, i * BLOCK:(i + 1) * BLOCK]
            norm = jnp.sqrt(jnp.sum(jnp.sum(gram * gram, axis=1, keepdims=True), axis=0, keepdims=True) + 1e-06)
            x_ref[g * PACK + i] = gram / norm

    def step(it, carry):
        for n in range(count):
            x = x_ref[n]
            square = lax.dot_general(
                x, x, (((1,), (1,)), ((), ())),
                precision=lax.Precision.HIGHEST, preferred_element_type=jnp.float32,
            )
            cube = jnp.dot(square, x, precision=lax.Precision.HIGHEST, preferred_element_type=jnp.float32)
            x_ref[n] = 1.5 * x - 0.5 * cube
        return carry

    lax.fori_loop(0, NS_STEPS, step, 0)
    for g in range(MINE):
        packed = jnp.concatenate([x_ref[g * PACK + i] for i in range(PACK)], axis=1).astype(o_ref.dtype)
        for s in range(SLICES):
            o_ref[s, g] = packed


def polars(parts):
    return pl.pallas_call(
        polar_kernel,
        in_specs=[VMEM],
        out_specs=VMEM,
        out_shape=jax.ShapeDtypeStruct((SLICES, MINE, BLOCK, LANES), jnp.bfloat16),
        scratch_shapes=[pltpu.VMEM((MINE * PACK, BLOCK, BLOCK), jnp.float32)],
    )(parts)


def align_kernel(cluster_ref, weight_ref, core_ref, own_ref, got_ref, w_ref, o_ref, acc_ref):
    acc_ref[...] = jnp.zeros_like(acc_ref)
    core = core_ref[0]

    def step(g, carry):
        for half, ref in ((core, own_ref), (1 - core, got_ref)):
            packed = ref[g]
            for i in range(PACK):
                p = (half * GROUPS + g) * PACK + i
                m = flip(p)
                turned = jnp.dot(
                    packed[:, i * BLOCK:(i + 1) * BLOCK], w_ref[p], preferred_element_type=jnp.float32
                )
                turned = (turned * weight_ref[m]).astype(jnp.bfloat16).astype(jnp.float32)
                k = cluster_ref[m]
                slot = (k >> 3) * 8 + (k & 1) * 4 + ((k >> 1) & 3)
                acc_ref[slot] = acc_ref[slot] + turned
        return carry

    lax.fori_loop(0, GROUPS, step, 0)
    o_ref[...] = acc_ref[...].astype(o_ref.dtype)


def align(cluster_ids, weight, core, own, got, columns):
    return pl.pallas_call(
        align_kernel,
        in_specs=[SMEM, SMEM, SMEM, VMEM, VMEM, VMEM],
        out_specs=VMEM,
        out_shape=jax.ShapeDtypeStruct((CLUSTERS, BLOCK, COLS), jnp.bfloat16),
        scratch_shapes=[pltpu.VMEM((CLUSTERS, BLOCK, COLS), jnp.float32)],
    )(cluster_ids, weight, core, own, got, columns)


def final_kernel(m_ref, o_ref):
    for c in range(NC):
        o_ref[0, :, c * COLS:(c + 1) * COLS] = m_ref[0, c]


def final(merged):
    rows = merged.shape[2]
    return pl.pallas_call(
        final_kernel,
        grid=(NX,),
        in_specs=[pl.BlockSpec((1, NC, rows, COLS), lambda x: (x, 0, 0, 0))],
        out_specs=pl.BlockSpec((1, rows, NC * COLS), lambda x: (0, x, 0)),
        out_shape=jax.ShapeDtypeStruct((1, NX * rows, NC * COLS), merged.dtype),
    )(merged)


def exchange(value, axes):
    return lax.all_to_all(value, axes, split_axis=0, concat_axis=0, tiled=True)


def on_device(w_up, cluster, counts):
    cluster_ids = cluster[:, 0]
    index = jnp.arange(EXPERTS, dtype=jnp.int32)
    labels = jnp.arange(CLUSTERS, dtype=jnp.int32)
    member = cluster_ids[None, :] == labels[:, None]
    score = counts * EXPERTS + (EXPERTS - 1 - index)
    best = jnp.max(jnp.where(member, score[None, :], -1), axis=1)
    leader = EXPERTS - 1 - best % EXPERTS
    anchor_of = jnp.sum(jnp.where(member, leader[:, None], 0), axis=0)
    total = jnp.sum(jnp.where(member, counts[None, :], 0), axis=1).astype(jnp.float32)
    weight = counts.astype(jnp.float32) / jnp.sum(jnp.where(member, total[:, None], 0.0), axis=0)
    core = lax.axis_index("core").astype(jnp.int32).reshape(1)

    got = lax.ppermute(spread(core, w_up, True), "core", SWAP)
    rows = join(core, got, spread(core, w_up, False))
    rows = rows.reshape(NZB * SLICES, -1, COLS)
    columns = exchange(rows, ("zb", "y", "zc")).reshape(EXPERTS, BLOCK, COLS)

    got = lax.ppermute(grams(anchor_of, core, columns, True), "core", SWAP)
    partial = grams(anchor_of, core, columns, False) + got
    parts = exchange(partial, ("y", "zc"))
    copies = polars(parts.reshape(SLICES, MINE, BLOCK, LANES))
    own = exchange(copies, ("y", "zc")).reshape(GROUPS, BLOCK, LANES)
    merged = align(cluster_ids, weight, core, own, lax.ppermute(own, "core", SWAP), columns)

    merged = exchange(merged, ("y", "zc", "zb"))
    merged = exchange(merged.reshape(SLICES, NZB * BLOCK, COLS), ("x", "core"))
    return final(merged.reshape(NX, NC, NZB * BLOCK, COLS))


def solution(mesh):
    grid = Mesh(mesh.devices.reshape(NY, NZB, NZC, NX, NC), ("y", "zb", "zc", "x", "core"))
    return jax.shard_map(
        on_device,
        mesh=grid,
        in_specs=(P(("y", "zb", "zc"), ("x", "core"), None), P(), P()),
        out_specs=P(("y", "zb", "zc"), None, ("x", "core")),
        check_vma=False,
    )
```

time: 402 us -> 368 us (0.915)
  waiting for transfers between devices: 231 us -> 142 us
  Pallas kernels: 29.3 us -> 77.4 us
  blocking collectives: 90.9 us -> 126 us
  matrix products: 14.5 us -> 0 us
  between operations: 13.6 us -> 0.06 us
  starting transfers between devices: 11.2 us -> 16 us
    pallas_call x3 -> x8, Pallas kernels: 29.3 us -> 77.4 us  [the longest x1 26.6 us: polars(): pl.pallas_call(polar_kernel, in_specs=[VMEM], out_specs=VMEM, out_shape=j...]
    reduce_scatter x1 -> x0, waiting for transfers between devices: 43.9 us -> none  [on_device(): gram = lax.psum_scatter(partial, 'z', scatter_dimension=0, tiled=True)]
    all_gather x1 -> x0, waiting for transfers between devices: 42.3 us -> none  [on_device(): polar = lax.all_gather(polar, ('z', 'core'), axis=0, tiled=True)]
    all_to_all x3 -> x4, blocking collectives: 90.9 us -> 126 us  [exchange(): return lax.all_to_all(value, axes, split_axis=0, concat_axis=0, tiled=True)]
    dot_general x16 -> x0, matrix products: 14.5 us -> none  [the longest x8 8.23 us: newton_schulz(): jnp.einsum('...ij,...kj->...ik', value, value, precision=lax.Precision.HI...]
    ppermute x1 -> x3, starting transfers between devices: 1.37 us -> 6.24 us  [the longest x1 3.2 us: on_device(): got = lax.ppermute(spread(core, w_up, True), 'core', SWAP)]
  transfers between devices with their start and end apart: 4 -> 4, of which waited for: 4 -> 2; matrix products, arithmetic and copies ran while one was open for 0% -> 0% of each run, Pallas kernels for 0% -> 4%
where the time goes in v2:
time: 368 us; the launch traced here: 367 us
  waiting for transfers between devices  142 us (39%)
  blocking collectives  126 us (34%)
  Pallas kernels  77.4 us (21%)
  starting transfers between devices  16 us (4%)
    all_to_all x1, waiting for transfers between devices, exchange(): return lax.all_to_all(value, axes, split_axis=0, concat_axis=0, tiled=True)  141 us
    all_to_all x4, blocking collectives, exchange(): return lax.all_to_all(value, axes, split_axis=0, concat_axis=0, tiled=True)  126 us
    pallas_call x1, Pallas kernels, polars(): pl.pallas_call(polar_kernel, in_specs=[VMEM], out_specs=VMEM, out_shape=j...  26.6 us
    pallas_call x2, Pallas kernels, grams(): pl.pallas_call(kernel, in_specs=[SMEM, SMEM, VMEM], out_specs=VMEM, out_s...  17.1 us
    pallas_call x2, Pallas kernels, spread(): pl.pallas_call(kernel, grid_spec=pltpu.PrefetchScalarGridSpec(num_scalar_...  13.8 us
    pallas_call x1, Pallas kernels, align(): pl.pallas_call(align_kernel, in_specs=[SMEM, SMEM, SMEM, VMEM, VMEM, VMEM...  10.1 us
    all_to_all x1, starting transfers between devices, exchange(): return lax.all_to_all(value, axes, split_axis=0, concat_axis=0, tiled=True)  9.74 us
  transfers between devices with their start and end apart: 4, of which 2 were waited for; matrix products, arithmetic and copies ran while one was open for 0% of the time, Pallas kernels for 4%

profile of v2, /device:TPU:1, one launch (start us, length us, event | category | flops | bytes accessed | tf_op | source)
XLA Modules:
  0.0 367.3 jit_solution(4251857175664470051)
XLA Ops:
  0.0 6.9 %shard_map.37 = bf16[2,8,4,96,256]{4,3,2,1,0:T(8,128)(2,1)} custom-call(s32[1]{0:T(128)} %bitcast.1.core_ref, bf16[4,192,4096]{2,1,0:T(8,128)(2,1)} %w_ref.3), custom_call_target="tpu_custom_call" | custom-call | tf_op jit(solution)/shard_map/pallas_call | solution.py:45
  6.9 3.2 collective-permute-start
  10.1 6.9 %shard_map.38.held_ref = bf16[4,8,4,96,256]{4,3,2,1,0:T(8,128)(2,1)} custom-call(s32[1]{0:T(128)} %bitcast.1.core_ref, bf16[4,192,4096]{2,1,0:T(8,128)(2,1)} %w_ref.3), custom_call_target="tpu_custom_call" | custom-call | tf_op jit(solution)/shard_map/pallas_call | solution.py:45
  17.0 1.7 copy-done.1
  18.7 6.2 %shard_map.39 = bf16[4,8,4,96,256]{4,3,2,1,0:T(8,128)(2,1)} custom-call(s32[1]{0:T(128)} %bitcast.1.core_ref, bf16[2,8,4,96,256]{4,3,2,1,0:T(8,128)(2,1)} %copy-done.1, bf16[4,8,4,96,256]{4,3,2,1,0:T(8,128)(2,1)} %shard_map.38.held_ref), custom_call_target="tpu_custom_call", output_to_operand_aliasing={{}: (2, {})} | custom-call | tf_op jit(solution)/shard_map/pallas_call | solution.py:64
  24.8 9.7 %all-to-all-start = ((bf16[32,384,256]{2,1,0:T(8,128)(2,1)}), bf16[32,384,256]{2,1,0:T(8,128)(2,1)}, u32[]{:S(2)}, u32[]{:S(2)}) async-start(bf16[32,384,256]{2,1,0:T(8,128)(2,1)} %bitcast.8), calls=%async_computation | async-start | bytes 12582912 | tf_op jit(solution)/shard_map/all_to_all | solution.py:196
  34.6 0.1 select_reduce_fusion.1
  34.7 0.6 select_reduce_fusion
  35.3 140.5 %all-to-all-done = bf16[32,384,256]{2,1,0:T(8,128)(2,1)} async-done(((bf16[32,384,256]{2,1,0:T(8,128)(2,1)}), bf16[32,384,256]{2,1,0:T(8,128)(2,1)}, u32[]{:S(2)}, u32[]{:S(2)}) %all-to-all-start) | async-done | bytes 6291488 | tf_op jit(solution)/shard_map/all_to_all | solution.py:196
  175.9 8.6 %shard_map.41 = f32[16,96,384]{2,1,0:T(8,128)} custom-call(s32[128]{0:T(128)} %get-tuple-element.5.anchor_ref, s32[1]{0:T(128)} %bitcast.1.core_ref, bf16[128,96,256]{2,1,0:T(8,128)(2,1)} %bitcast.3.w_ref), custom_call_target="tpu_custom_call" | custom-call | tf_op jit(solution)/shard_map/pallas_call | solution.py:99
  184.4 1.0 collective-permute-start.1
  185.5 8.5 %shard_map.40 = f32[16,96,384]{2,1,0:T(8,128)} custom-call(s32[128]{0:T(128)} %get-tuple-element.5.anchor_ref, s32[1]{0:T(128)} %bitcast.1.core_ref, bf16[128,96,256]{2,1,0:T(8,128)(2,1)} %bitcast.3.w_ref), custom_call_target="tpu_custom_call" | custom-call | tf_op jit(solution)/shard_map/pallas_call | solution.py:99
  194.0 1.9 add.18
  195.9 35.6 %all_to_all.25 = f32[16,96,384]{2,1,0:T(8,128)} all-to-all(f32[16,96,384]{2,1,0:T(8,128)S(1)} %add.18), channel_id=1, replica_groups=mesh['y'=4,'zb'=4,'zc'=2,'x'=4,'core'=2] {'y','zc'}, dimensions={0} | all-to-all | bytes 4718592 | tf_op jit(solution)/shard_map/all_to_all | solution.py:196
  231.5 26.6 %shard_map.42 = bf16[8,2,96,384]{3,2,1,0:T(8,128)(2,1)} custom-call(f32[8,2,96,384]{3,2,1,0:T(8,128)} %bitcast.9), custom_call_target="tpu_custom_call" | custom-call | tf_op jit(solution)/shard_map/pallas_call | solution.py:137
  258.1 19.7 %all_to_all.26 = bf16[8,2,96,384]{3,2,1,0:T(8,128)(2,1)S(1)} all-to-all(bf16[8,2,96,384]{3,2,1,0:T(8,128)(2,1)} %shard_map.42), channel_id=1, replica_groups=mesh['y'=4,'zb'=4,'zc'=2,'x'=4,'core'=2] {'y','zc'}, dimensions={0} | all-to-all | bytes 2359296 | tf_op jit(solution)/shard_map/all_to_all | solution.py:196
  277.8 2.0 collective-permute-start.2
  279.9 0.5 convert_divide_fusion.weight_ref
  280.4 1.8 collective-permute-done.2.got_ref
  282.3 1.1 copy-done.2
  283.3 10.1 %shard_map.43 = bf16[32,96,256]{2,1,0:T(8,128)(2,1)} custom-call(s32[128]{0:T(128)} %bitcast.14, f32[128]{0:T(128)} %convert_divide_fusion.weight_ref, s32[1]{0:T(128)} %bitcast.1.core_ref, bf16[16,96,384]{2,1,0:T(8,128)(2,1)} %bitcast.13, bf16[16,96,384]{2,1,0:T(8,128)(2,1)} %copy-done.2, bf16[128,96,256]{2,1,0:T(8,128)(2,1)} %bitcast.3.w_ref), custom_call_target="tpu_custom_call" | custom-call | tf_op jit(solution)/shard_map/pallas_call | solution.py:170
  293.5 42.5 %all_to_all.27 = bf16[32,96,256]{2,1,0:T(8,128)(2,1)S(1)} all-to-all(bf16[32,96,256]{2,1,0:T(8,128)(2,1)} %shard_map.43), channel_id=1, replica_groups=mesh['y'=4,'zb'=4,'zc'=2,'x'=4,'core'=2] {'y','zc','zb'}, dimensions={0} | all-to-all | bytes 3145728 | tf_op jit(solution)/shard_map/all_to_all | solution.py:196
  335.9 27.8 %all_to_all.28 = bf16[8,384,256]{2,1,0:T(8,128)(2,1)} all-to-all(bf16[8,384,256]{2,1,0:T(8,128)(2,1)S(1)} %bitcast.10), channel_id=1, replica_groups=mesh['y'=4,'zb'=4,'zc'=2,'x'=4,'core'=2] {'x','core'}, dimensions={0} | all-to-all | bytes 3145728 | tf_op jit(solution)/shard_map/all_to_all | solution.py:196
  363.8 3.6 shard_map.44
  (14 shorter events, 0.1 us)
Async XLA Ops:
  6.9 10.1 %collective-permute-start = (bf16[2,8,4,96,256]{4,3,2,1,0:T(8,128)(2,1)}, bf16[2,8,4,96,256]{4,3,2,1,0:T(8,128)(2,1)S(1)}, u32[]{:S(2)}, u32[]{:S(2)}) collective-permute-start(bf16[2,8,4,96,256]{4,3,2,1,0:T(8,128)(2,1)} %shard_map.37), channel_id=1, source_target_pairs={{0,1},{1,0},{2,3},{3,2},{4,5},{5,4},{6,7},{7,6},{8,9},{9,8},{10,11... | collective-permute-start | bytes 9437192 | tf_op jit(solution)/shard_map/ppermute | solution.py:212
  17.0 1.7 copy-start.1
  24.8 9.8 %copy-start.4 = (s32[128]{0:T(128)S(1)}, s32[128]{0:T(128)}, u32[]{:S(2)}) copy-start(s32[128]{0:T(128)} %param.5) | copy-start | bytes 1540
  24.8 9.8 %copy-start.3 = (s32[128,1]{0,1:T(1,128)S(1)}, s32[128,1]{0,1:T(1,128)}, u32[]{:S(2)}) copy-start(s32[128,1]{0,1:T(1,128)} %param.4) | copy-start | bytes 1540
  24.8 151.0 %all-to-all-start = ((bf16[32,384,256]{2,1,0:T(8,128)(2,1)}), bf16[32,384,256]{2,1,0:T(8,128)(2,1)}, u32[]{:S(2)}, u32[]{:S(2)}) async-start(bf16[32,384,256]{2,1,0:T(8,128)(2,1)} %bitcast.8), calls=%async_computation | async-start | bytes 12582912 | tf_op jit(solution)/shard_map/all_to_all | solution.py:196
  184.4 9.6 %collective-permute-start.1 = (f32[16,96,384]{2,1,0:T(8,128)}, f32[16,96,384]{2,1,0:T(8,128)S(1)}, u32[]{:S(2)}, u32[]{:S(2)}) collective-permute-start(f32[16,96,384]{2,1,0:T(8,128)} %shard_map.41), channel_id=1, source_target_pairs={{0,1},{1,0},{2,3},{3,2},{4,5},{5,4},{6,7},{7,6},{8,9},{9,8},{10,11... | collective-permute-start | bytes 7077896 | tf_op jit(solution)/shard_map/ppermute | solution.py:217
  277.8 4.5 %copy-start = (bf16[8,2,96,384]{3,2,1,0:T(8,128)(2,1)}, bf16[8,2,96,384]{3,2,1,0:T(8,128)(2,1)S(1)}, u32[]{:S(2)}) copy-start(bf16[8,2,96,384]{3,2,1,0:T(8,128)(2,1)S(1)} %all_to_all.26) | copy-start | bytes 3538948
  277.8 4.5 %collective-permute-start.2 = (bf16[16,96,384]{2,1,0:T(8,128)(2,1)S(1)}, bf16[16,96,384]{2,1,0:T(8,128)(2,1)S(1)}, u32[]{:S(2)}, u32[]{:S(2)}) collective-permute-start(bf16[16,96,384]{2,1,0:T(8,128)(2,1)S(1)} %bitcast.12), channel_id=1, source_target_pairs={{0,1},{1,0},{2,3},{3,2},{4,5},{5,4},{6,7},{7,6},{8,9},{9,8},{10,11... | collective-permute-start | bytes 3538952 | tf_op jit(solution)/shard_map/ppermute | solution.py:222
  282.3 1.1 copy-start.2

commit v3 on v2

v3 whole, which is shorter than its diff:
```python
import jax
import jax.numpy as jnp
from jax import lax
from jax.experimental import pallas as pl
from jax.experimental.pallas import tpu as pltpu
from jax.sharding import Mesh, PartitionSpec as P

BLOCK = 96
NS_STEPS = 8
NY, NZB, NZC, NX, NC = 4, 4, 2, 4, 2
EXPERTS = 128
CLUSTERS = 32
COLS = 256
PACK = 4
LANE = 128
LANES = PACK * BLOCK
SLICES = NY * NZC
GROUPS = EXPERTS // PACK // NC
MINE = GROUPS // SLICES
SWAP = [(0, 1), (1, 0)]
VMEM = pl.BlockSpec(memory_space=pltpu.VMEM)
SMEM = pl.BlockSpec(memory_space=pltpu.SMEM)
ANY = pl.BlockSpec(memory_space=pl.ANY)
NT = (((1,), (1,)), ((), ()))
SMALL = pltpu.CompilerParams(vmem_limit_bytes=20 * 2**20)


def flip(position):
    return ((position >> 3) & 3) * 32 + (position >> 5) * 8 + (position & 7)


def quarters(parts):
    lane = lax.broadcasted_iota(jnp.int32, parts[0].shape, 1)
    low = lane < 64
    even = (lane // 32) % 2 == 0
    first = [jnp.where(low, parts[t], pltpu.roll(parts[t + 2], 64, 1)) for t in range(2)]
    second = [jnp.where(low, pltpu.roll(parts[t], 64, 1), parts[t + 2]) for t in range(2)]
    out = []
    for one, two in (first, second):
        out.append(jnp.where(even, one, pltpu.roll(two, 32, 1)))
        out.append(jnp.where(even, pltpu.roll(one, 96, 1), two))
    return out


def spread_kernel(core_ref, w_ref, held_ref, send_ref):
    def go(core):
        for h in range(2):
            for a in range(4):
                starts = [(4 * h + t) * 4 * LANE + a * LANE for t in range(4)]
                pieces = quarters([w_ref[0, :, s:s + LANE] for s in starts])
                for b in range(4):
                    ref = held_ref if b % 2 == core else send_ref
                    ref[0, 2 * a + b // 2, 0, :, h * LANE:(h + 1) * LANE] = pieces[b]

    for core in range(NC):
        pl.when(core_ref[0] == core)(lambda core=core: go(core))


def spread(core, w):
    experts, units, width = w.shape
    blocks = units // BLOCK
    block = (1, SLICES, 1, BLOCK, COLS)
    return pl.pallas_call(
        spread_kernel,
        compiler_params=SMALL,
        grid_spec=pltpu.PrefetchScalarGridSpec(
            num_scalar_prefetch=1,
            grid=(experts, blocks),
            in_specs=[pl.BlockSpec((1, BLOCK, width), lambda e, j, core_ref: (e, j, 0))],
            out_specs=[
                pl.BlockSpec(block, lambda e, j, core_ref: (core_ref[0] * blocks + j, 0, e, 0, 0)),
                pl.BlockSpec(block, lambda e, j, core_ref: (j, 0, e, 0, 0)),
            ],
        ),
        out_shape=[
            jax.ShapeDtypeStruct((NC * blocks, SLICES, experts, BLOCK, COLS), w.dtype),
            jax.ShapeDtypeStruct((blocks, SLICES, experts, BLOCK, COLS), w.dtype),
        ],
    )(core, w)


def join_kernel(core_ref, got_ref, held_ref, o_ref, sem):
    blocks = got_ref.shape[0]
    copy = pltpu.make_async_copy(got_ref, o_ref.at[pl.ds((1 - core_ref[0]) * blocks, blocks)], sem)
    copy.start()
    copy.wait()


def join(core, got, held):
    return pl.pallas_call(
        join_kernel,
        compiler_params=SMALL,
        in_specs=[SMEM, ANY, ANY],
        out_specs=ANY,
        out_shape=jax.ShapeDtypeStruct(held.shape, held.dtype),
        scratch_shapes=[pltpu.SemaphoreType.DMA],
        input_output_aliases={2: 0},
    )(core, got, held)


def grams(anchor_of, core, columns, other):
    def kernel(anchor_ref, core_ref, w_ref, o_ref):
        half = 1 - core_ref[0] if other else core_ref[0]

        def step(g, carry):
            parts = []
            for i in range(PACK):
                p = (half * GROUPS + g) * PACK + i
                lead = flip(anchor_ref[flip(p)])
                parts.append(lax.dot_general(w_ref[lead], w_ref[p], NT, preferred_element_type=jnp.float32))
            o_ref[g] = jnp.concatenate(parts, axis=1)
            return carry

        lax.fori_loop(0, GROUPS, step, 0, unroll=4)

    return pl.pallas_call(
        kernel,
        compiler_params=SMALL,
        in_specs=[SMEM, SMEM, VMEM],
        out_specs=VMEM,
        out_shape=jax.ShapeDtypeStruct((GROUPS, BLOCK, LANES), jnp.float32),
    )(anchor_of, core, columns)


def split(value):
    high = value.astype(jnp.bfloat16)
    return high, (value - high.astype(jnp.float32)).astype(jnp.bfloat16)


def fold(product):
    return product[:BLOCK, :LANE] + product[BLOCK:, :LANE] + product[:BLOCK, LANE:]


def polar_kernel(part_ref, o_ref, x_ref):
    count = MINE * PACK
    for g in range(MINE):
        total = part_ref[0, g]
        for s in range(1, SLICES):
            total = total + part_ref[s, g]
        for i in range(PACK):
            gram = total[:, i * BLOCK:(i + 1) * BLOCK]
            gram = jnp.concatenate([gram, jnp.zeros((BLOCK, LANE - BLOCK), jnp.float32)], axis=1)
            norm = jnp.sqrt(jnp.sum(jnp.sum(gram * gram, axis=1, keepdims=True), axis=0, keepdims=True) + 1e-06)
            x_ref[g * PACK + i] = gram / norm
    pad = jnp.zeros((LANE - BLOCK, LANE), jnp.bfloat16)

    def square(high, low):
        return lax.dot_general(
            jnp.concatenate([high, low], 0), jnp.concatenate([high, pad, low, pad], 0), NT,
            preferred_element_type=jnp.float32,
        )

    def times(one, two):
        wide = jnp.concatenate([jnp.concatenate([part, pad], 0) for part in two], 1)
        return jnp.dot(jnp.concatenate(one, 0), wide, preferred_element_type=jnp.float32)

    def step(it, carry):
        values = [x_ref[n] for n in range(count)]
        halves = [split(v) for v in values]
        squares = [split(fold(square(*v))) for v in halves]
        cubes = [times(s, v) for s, v in zip(squares, halves)]
        for n in range(count):
            x_ref[n] = 1.5 * values[n] - 0.5 * fold(cubes[n])
        return carry

    lax.fori_loop(0, NS_STEPS, step, 0)
    for g in range(MINE):
        packed = jnp.concatenate([x_ref[g * PACK + i][:, :BLOCK] for i in range(PACK)], axis=1).astype(o_ref.dtype)
        for s in range(SLICES):
            o_ref[s, g] = packed


def polars(parts):
    return pl.pallas_call(
        polar_kernel,
        compiler_params=SMALL,
        in_specs=[VMEM],
        out_specs=VMEM,
        out_shape=jax.ShapeDtypeStruct((SLICES, MINE, BLOCK, LANES), jnp.bfloat16),
        scratch_shapes=[pltpu.VMEM((MINE * PACK, BLOCK, LANE), jnp.float32)],
    )(parts)


def align_kernel(cluster_ref, weight_ref, core_ref, own_ref, got_ref, w_ref, o_ref, acc_ref):
    acc_ref[...] = jnp.zeros_like(acc_ref)
    core = core_ref[0]

    def step(g, carry):
        for half, ref in ((core, own_ref), (1 - core, got_ref)):
            packed = ref[g]
            turned = []
            for i in range(PACK):
                p = (half * GROUPS + g) * PACK + i
                part = jnp.dot(packed[:, i * BLOCK:(i + 1) * BLOCK], w_ref[p], preferred_element_type=jnp.float32)
                turned.append((part * weight_ref[flip(p)]).astype(jnp.bfloat16).astype(jnp.float32))
            for i in range(PACK):
                k = cluster_ref[flip((half * GROUPS + g) * PACK + i)]
                acc_ref[k] = acc_ref[k] + turned[i]
        return carry

    lax.fori_loop(0, GROUPS, step, 0, unroll=4)
    rows = BLOCK // 4

    def put(k, carry):
        for h in range(2):
            pieces = quarters([acc_ref[k, q * rows:(q + 1) * rows, h * LANE:(h + 1) * LANE] for q in range(4)])
            for t in range(4):
                o_ref[4 * h + t, k] = pieces[t].astype(o_ref.dtype)
        return carry

    lax.fori_loop(0, CLUSTERS, put, 0, unroll=2)


def align(cluster_ids, weight, core, own, got, columns):
    return pl.pallas_call(
        align_kernel,
        compiler_params=SMALL,
        in_specs=[SMEM, SMEM, SMEM, VMEM, VMEM, VMEM],
        out_specs=VMEM,
        out_shape=jax.ShapeDtypeStruct((NX * NC, CLUSTERS, BLOCK // 4, LANE), jnp.bfloat16),
        scratch_shapes=[pltpu.VMEM((CLUSTERS, BLOCK, COLS), jnp.float32)],
    )(cluster_ids, weight, core, own, got, columns)


def final_kernel(m_ref, o_ref):
    for zb in range(NZB):
        for a in range(4):
            pieces = quarters([m_ref[0, b % 2, a, zb, b // 2] for b in range(4)])
            o_ref[0, zb * BLOCK:(zb + 1) * BLOCK, a * LANE:(a + 1) * LANE] = jnp.concatenate(pieces, 0)


def final(merged):
    rows = NZB * BLOCK
    return pl.pallas_call(
        final_kernel,
        compiler_params=SMALL,
        grid=(NX,),
        in_specs=[pl.BlockSpec((1,) + merged.shape[1:], lambda x: (x,) + (0,) * 6)],
        out_specs=pl.BlockSpec((1, rows, NC * COLS), lambda x: (0, x, 0)),
        out_shape=jax.ShapeDtypeStruct((1, NX * rows, NC * COLS), merged.dtype),
    )(merged)


def exchange(value, axes):
    return lax.all_to_all(value, axes, split_axis=0, concat_axis=0, tiled=True)


def on_device(w_up, cluster, counts):
    cluster_ids = cluster[:, 0]
    index = jnp.arange(EXPERTS, dtype=jnp.int32)
    labels = jnp.arange(CLUSTERS, dtype=jnp.int32)
    member = cluster_ids[None, :] == labels[:, None]
    score = counts * EXPERTS + (EXPERTS - 1 - index)
    best = jnp.max(jnp.where(member, score[None, :], -1), axis=1)
    leader = EXPERTS - 1 - best % EXPERTS
    anchor_of = jnp.sum(jnp.where(member, leader[:, None], 0), axis=0)
    total = jnp.sum(jnp.where(member, counts[None, :], 0), axis=1).astype(jnp.float32)
    weight = counts.astype(jnp.float32) / jnp.sum(jnp.where(member, total[:, None], 0.0), axis=0)
    core = lax.axis_index("core").astype(jnp.int32).reshape(1)

    held, send = spread(core, w_up)
    rows = join(core, lax.ppermute(send, "core", SWAP), held)
    rows = rows.reshape(NZB * SLICES, -1, COLS)
    rows, anchor_of, weight = lax.optimization_barrier((rows, anchor_of, weight))
    columns = exchange(rows, ("zb", "y", "zc")).reshape(EXPERTS, BLOCK, COLS)

    got = lax.ppermute(grams(anchor_of, core, columns, True), "core", SWAP)
    partial = grams(anchor_of, core, columns, False) + got
    parts = exchange(partial, ("y", "zc"))
    copies = polars(parts.reshape(SLICES, MINE, BLOCK, LANES))
    own = exchange(copies, ("y", "zc")).reshape(GROUPS, BLOCK, LANES)
    merged = align(cluster_ids, weight, core, own, lax.ppermute(own, "core", SWAP), columns)

    merged = exchange(merged.reshape(-1, BLOCK // 4, LANE), ("x", "core", "y", "zb", "zc"))
    return final(merged.reshape(NX, NC, NY, NZB, NZC, BLOCK // 4, LANE))


def solution(mesh):
    grid = Mesh(mesh.devices.reshape(NY, NZB, NZC, NX, NC), ("y", "zb", "zc", "x", "core"))
    return jax.shard_map(
        on_device,
        mesh=grid,
        in_specs=(P(("y", "zb", "zc"), ("x", "core"), None), P(), P()),
        out_specs=P(("y", "zb", "zc"), None, ("x", "core")),
        check_vma=False,
    )
```

time: 368 us -> 300 us (0.82)
  waiting for transfers between devices: 142 us -> 9.29 us
  blocking collectives: 126 us -> 251 us
  Pallas kernels: 77.4 us -> 28.5 us
  starting transfers between devices: 16 us -> 7.13 us
    all_to_all x1 -> x0, waiting for transfers between devices: 141 us -> none  [exchange(): return lax.all_to_all(value, axes, split_axis=0, concat_axis=0, tiled=True)]
    all_to_all x4, blocking collectives: 126 us -> 251 us  [exchange(): return lax.all_to_all(value, axes, split_axis=0, concat_axis=0, tiled=True)]
    pallas_call x8 -> x7, Pallas kernels: 77.4 us -> 28.5 us  [the longest x1 7.5 us: spread(): pl.pallas_call(spread_kernel, compiler_params=SMALL, grid_spec=pltpu.Pref...]
    all_to_all x1 -> x0, starting transfers between devices: 9.74 us -> none  [exchange(): return lax.all_to_all(value, axes, split_axis=0, concat_axis=0, tiled=True)]
    ppermute x1, waiting for transfers between devices: 0.01 us -> 4.92 us  [on_device(): rows = join(core, lax.ppermute(send, 'core', SWAP), held)]
  transfers between devices with their start and end apart: 4 -> 3, of which waited for: 2 -> 3; matrix products, arithmetic and copies ran while one was open for 0% -> 0% of each run, Pallas kernels for 4% -> 1%
where the time goes in v3:
time: 300 us; the launch traced here: 299 us
  blocking collectives  251 us (84%)
  Pallas kernels  28.5 us (10%)
  waiting for transfers between devices  9.29 us (3%)
  starting transfers between devices  7.13 us (2%)
    all_to_all x4, blocking collectives, exchange(): return lax.all_to_all(value, axes, split_axis=0, concat_axis=0, tiled=True)  251 us
    pallas_call x1, Pallas kernels, spread(): pl.pallas_call(spread_kernel, compiler_params=SMALL, grid_spec=pltpu.Pref...  7.5 us
    pallas_call x1, Pallas kernels, align(): pl.pallas_call(align_kernel, compiler_params=SMALL, in_specs=[SMEM, SMEM,...  6.25 us
    pallas_call x1, Pallas kernels, polars(): pl.pallas_call(polar_kernel, compiler_params=SMALL, in_specs=[VMEM], out_...  6.05 us
  transfers between devices with their start and end apart: 3, of which 3 were waited for; matrix products, arithmetic and copies ran while one was open for 0% of the time, Pallas kernels for 1%

profile of v3, /device:TPU:1, one launch (start us, length us, event | category | flops | bytes accessed | tf_op | source)
XLA Modules:
  0.0 299.4 jit_solution(15188266070885127623)
XLA Ops:
  0.0 2.8 copy-done
  2.8 7.5 %shard_map.37 = (bf16[4,8,4,96,256]{4,3,2,1,0:T(8,128)(2,1)S(1)}, bf16[2,8,4,96,256]{4,3,2,1,0:T(8,128)(2,1)S(1)}) custom-call(s32[1]{0:T(128)} %bitcast.1.core_ref, bf16[4,192,4096]{2,1,0:T(8,128)(2,1)S(1)} %copy-done), custom_call_target="tpu_custom_call" | custom-call | tf_op jit(solution)/shard_map/pallas_call | solution.py:63
  10.3 3.3 %collective-permute-start = (bf16[2,8,4,96,256]{4,3,2,1,0:T(8,128)(2,1)S(1)}, bf16[2,8,4,96,256]{4,3,2,1,0:T(8,128)(2,1)S(1)}, u32[]{:S(2)}, u32[]{:S(2)}) collective-permute-start(bf16[2,8,4,96,256]{4,3,2,1,0:T(8,128)(2,1)S(1)} %get-tuple-element.10), channel_id=1, source_target_pairs={{0,1},{1,0},{2,3},{3,2},{4,5},{5,4},{6,7},{7,6},{8,9},{9,8},{10,11... | collective-permute-start | bytes 9437192 | tf_op jit(solution)/shard_map/ppermute | solution.py:262
  13.6 0.0 copy-done.2
  13.6 0.0 copy-done.1
  13.6 0.1 select_reduce_fusion.3
  13.7 0.1 select_reduce_fusion.1
  13.9 0.1 select_reduce_fusion
  14.0 4.9 %collective-permute-done.got_ref = bf16[2,8,4,96,256]{4,3,2,1,0:T(8,128)(2,1)S(1)} collective-permute-done((bf16[2,8,4,96,256]{4,3,2,1,0:T(8,128)(2,1)S(1)}, bf16[2,8,4,96,256]{4,3,2,1,0:T(8,128)(2,1)S(1)}, u32[]{:S(2)}, u32[]{:S(2)}) %collective-permute-start) | collective-permute-done | bytes 3145760 | tf_op jit(solution)/shard_map/ppermute | solution.py:262
  18.9 0.2 shard_map.38
  19.1 148.8 %all_to_all.20 = bf16[32,384,256]{2,1,0:T(8,128)(2,1)S(1)} all-to-all(bf16[32,384,256]{2,1,0:T(8,128)(2,1)S(1)} %bitcast.11), channel_id=1, replica_groups=mesh['y'=4,'zb'=4,'zc'=2,'x'=4,'core'=2] {'zb','y','zc'}, dimensions={0} | all-to-all | bytes 12582912 | tf_op jit(solution)/shard_map/all_to_all | solution.py:245
  167.9 2.3 shard_map.40
  170.2 1.4 collective-permute-start.1
  171.6 2.3 shard_map.39
  173.9 1.9 collective-permute-done.1
  175.8 0.3 add.18
  176.1 33.5 %all_to_all.21 = f32[16,96,384]{2,1,0:T(8,128)S(1)} all-to-all(f32[16,96,384]{2,1,0:T(8,128)S(1)} %add.18), channel_id=1, replica_groups=mesh['y'=4,'zb'=4,'zc'=2,'x'=4,'core'=2] {'y','zc'}, dimensions={0} | all-to-all | bytes 4718592 | tf_op jit(solution)/shard_map/all_to_all | solution.py:245
  209.6 6.0 %shard_map.41 = bf16[8,2,96,384]{3,2,1,0:T(8,128)(2,1)S(1)} custom-call(f32[8,2,96,384]{3,2,1,0:T(8,128)S(1)} %bitcast.12), custom_call_target="tpu_custom_call" | custom-call | tf_op jit(solution)/shard_map/pallas_call | solution.py:174
  215.7 18.7 %all_to_all.22 = bf16[8,2,96,384]{3,2,1,0:T(8,128)(2,1)S(1)} all-to-all(bf16[8,2,96,384]{3,2,1,0:T(8,128)(2,1)S(1)} %shard_map.41), channel_id=1, replica_groups=mesh['y'=4,'zb'=4,'zc'=2,'x'=4,'core'=2] {'y','zc'}, dimensions={0} | all-to-all | bytes 2359296 | tf_op jit(solution)/shard_map/all_to_all | solution.py:245
  234.3 2.4 collective-permute-start.2
  236.7 2.5 collective-permute-done.2.got_ref
  239.2 6.2 %shard_map.42 = bf16[8,32,24,128]{3,2,1,0:T(8,128)(2,1)S(1)} custom-call(s32[128]{0:T(128)S(1)} %bitcast.20, f32[128]{0:T(128)S(1)} %convert_divide_fusion.weight_ref, s32[1]{0:T(128)} %bitcast.1.core_ref, bf16[16,96,384]{2,1,0:T(8,128)(2,1)S(1)} %bitcast.16, bf16[16,96,384]{2,1,0:T(8,128)(2,1)S(1)} %collective-permute-done.2.got_ref, ...), custom_call_target="tpu_custom_call" | custom-call | tf_op jit(solution)/shard_map/pallas_call | solution.py:215
  245.5 49.9 %all_to_all.23 = bf16[256,24,128]{2,1,0:T(8,128)(2,1)S(1)} all-to-all(bf16[256,24,128]{2,1,0:T(8,128)(2,1)S(1)} %bitcast.14), channel_id=1, replica_groups=mesh['y'=4,'zb'=4,'zc'=2,'x'=4,'core'=2] {'x','core','y','zb','zc'}, dimensions={0} | all-to-all | bytes 3145728 | tf_op jit(solution)/shard_map/all_to_all | solution.py:245
  295.4 4.0 %shard_map.43 = bf16[1,1536,512]{2,1,0:T(8,128)(2,1)} custom-call(bf16[4,2,4,4,2,24,128]{6,5,4,3,2,1,0:T(8,128)(2,1)S(1)} %bitcast.13), custom_call_target="tpu_custom_call" | custom-call | tf_op jit(solution)/shard_map/pallas_call | solution.py:234
  (7 shorter events, 0.0 us)
Async XLA Ops:
  0.0 2.8 copy-start
  2.8 10.8 %copy-start.2 = (s32[128]{0:T(128)S(1)}, s32[128]{0:T(128)}, u32[]{:S(2)}) copy-start(s32[128]{0:T(128)} %param.5) | copy-start | bytes 1540
  2.8 10.8 %copy-start.1 = (s32[128,1]{0,1:T(1,128)S(1)}, s32[128,1]{0,1:T(1,128)}, u32[]{:S(2)}) copy-start(s32[128,1]{0,1:T(1,128)} %param.4) | copy-start | bytes 1540
  10.3 8.6 %collective-permute-start = (bf16[2,8,4,96,256]{4,3,2,1,0:T(8,128)(2,1)S(1)}, bf16[2,8,4,96,256]{4,3,2,1,0:T(8,128)(2,1)S(1)}, u32[]{:S(2)}, u32[]{:S(2)}) collective-permute-start(bf16[2,8,4,96,256]{4,3,2,1,0:T(8,128)(2,1)S(1)} %get-tuple-element.10), channel_id=1, source_target_pairs={{0,1},{1,0},{2,3},{3,2},{4,5},{5,4},{6,7},{7,6},{8,9},{9,8},{10,11... | collective-permute-start | bytes 9437192 | tf_op jit(solution)/shard_map/ppermute | solution.py:262
  170.2 5.6 %collective-permute-start.1 = (f32[16,96,384]{2,1,0:T(8,128)S(1)}, f32[16,96,384]{2,1,0:T(8,128)S(1)}, u32[]{:S(2)}, u32[]{:S(2)}) collective-permute-start(f32[16,96,384]{2,1,0:T(8,128)S(1)} %shard_map.40), channel_id=1, source_target_pairs={{0,1},{1,0},{2,3},{3,2},{4,5},{5,4},{6,7},{7,6},{8,9},{9,8},{10,11... | collective-permute-start | bytes 7077896 | tf_op jit(solution)/shard_map/ppermute | solution.py:267
  234.3 4.9 %collective-permute-start.2 = (bf16[16,96,384]{2,1,0:T(8,128)(2,1)S(1)}, bf16[16,96,384]{2,1,0:T(8,128)(2,1)S(1)}, u32[]{:S(2)}, u32[]{:S(2)}) collective-permute-start(bf16[16,96,384]{2,1,0:T(8,128)(2,1)S(1)} %bitcast.15), channel_id=1, source_target_pairs={{0,1},{1,0},{2,3},{3,2},{4,5},{5,4},{6,7},{7,6},{8,9},{9,8},{10,11... | collective-permute-start | bytes 3538952 | tf_op jit(solution)/shard_map/ppermute | solution.py:272

commit v4 on v3

--- a/solution.py
+++ b/solution.py
@@ -15,6 +15,7 @@
 LANE = 128
 LANES = PACK * BLOCK
 SLICES = NY * NZC
+SCALE = 8192.0
 GROUPS = EXPERTS // PACK // NC
 MINE = GROUPS // SLICES
 SWAP = [(0, 1), (1, 0)]
@@ -29,53 +30,39 @@
     return ((position >> 3) & 3) * 32 + (position >> 5) * 8 + (position & 7)
 
 
-def quarters(parts):
-    lane = lax.broadcasted_iota(jnp.int32, parts[0].shape, 1)
-    low = lane < 64
-    even = (lane // 32) % 2 == 0
-    first = [jnp.where(low, parts[t], pltpu.roll(parts[t + 2], 64, 1)) for t in range(2)]
-    second = [jnp.where(low, pltpu.roll(parts[t], 64, 1), parts[t + 2]) for t in range(2)]
-    out = []
-    for one, two in (first, second):
-        out.append(jnp.where(even, one, pltpu.roll(two, 32, 1)))
-        out.append(jnp.where(even, pltpu.roll(one, 96, 1), two))
-    return out
-
-
-def spread_kernel(core_ref, w_ref, held_ref, send_ref):
-    def go(core):
-        for h in range(2):
-            for a in range(4):
-                starts = [(4 * h + t) * 4 * LANE + a * LANE for t in range(4)]
-                pieces = quarters([w_ref[0, :, s:s + LANE] for s in starts])
-                for b in range(4):
-                    ref = held_ref if b % 2 == core else send_ref
-                    ref[0, 2 * a + b // 2, 0, :, h * LANE:(h + 1) * LANE] = pieces[b]
-
-    for core in range(NC):
-        pl.when(core_ref[0] == core)(lambda core=core: go(core))
-
-
-def spread(core, w):
+def halves(first, second):
+    low = lax.broadcasted_iota(jnp.int32, first.shape, 1) < LANE // 2
+    return (
+        jnp.where(low, first, pltpu.roll(second, LANE // 2, 1)),
+        jnp.where(low, pltpu.roll(first, LANE // 2, 1), second),
+    )
+
+
+def spread(core, w, other):
     experts, units, width = w.shape
     blocks = units // BLOCK
-    block = (1, SLICES, 1, BLOCK, COLS)
-    return pl.pallas_call(
-        spread_kernel,
-        compiler_params=SMALL,
-        grid_spec=pltpu.PrefetchScalarGridSpec(
-            num_scalar_prefetch=1,
-            grid=(experts, blocks),
-            in_specs=[pl.BlockSpec((1, BLOCK, width), lambda e, j, core_ref: (e, j, 0))],
-            out_specs=[
-                pl.BlockSpec(block, lambda e, j, core_ref: (core_ref[0] * blocks + j, 0, e, 0, 0)),
-                pl.BlockSpec(block, lambda e, j, core_ref: (j, 0, e, 0, 0)),
-            ],
-        ),
-        out_shape=[
-            jax.ShapeDtypeStruct((NC * blocks, SLICES, experts, BLOCK, COLS), w.dtype),
-            jax.ShapeDtypeStruct((blocks, SLICES, experts, BLOCK, COLS), w.dtype),
-        ],
+    span = width // NX
+
+    def kernel(core_ref, w_ref, o_ref):
+        half = 1 - core_ref[0] if other else core_ref[0]
+        base = 0 if other else half * blocks
+        for e in range(experts):
+            for j in range(blocks):
+                rows = slice(j * BLOCK, (j + 1) * BLOCK)
+                for h in range(NX // 2):
+                    for a in range(SLICES // 2):
+                        starts = [(2 * h + t) * span + half * (span // NC) + a * LANE for t in range(2)]
+                        pair = halves(*[w_ref[e, rows, pl.ds(pl.multiple_of(s, LANE), LANE)] for s in starts])
+                        for b in range(2):
+                            o_ref[base + j, 2 * a + b, e, :, h * LANE:(h + 1) * LANE] = pair[b]
+
+    shape = (blocks if other else NC * blocks, SLICES, experts, BLOCK, COLS)
+    return pl.pallas_call(
+        kernel,
+        compiler_params=SMALL,
+        in_specs=[SMEM, VMEM],
+        out_specs=VMEM,
+        out_shape=jax.ShapeDtypeStruct(shape, w.dtype),
     )(core, w)
 
 
@@ -137,6 +124,7 @@
         total = part_ref[0, g]
         for s in range(1, SLICES):
             total = total + part_ref[s, g]
+        total = total * (1.0 / SCALE)
         for i in range(PACK):
             gram = total[:, i * BLOCK:(i + 1) * BLOCK]
             gram = jnp.concatenate([gram, jnp.zeros((BLOCK, LANE - BLOCK), jnp.float32)], axis=1)
@@ -199,13 +187,13 @@
         return carry
 
     lax.fori_loop(0, GROUPS, step, 0, unroll=4)
-    rows = BLOCK // 4
+    rows = BLOCK // 2
 
     def put(k, carry):
-        for h in range(2):
-            pieces = quarters([acc_ref[k, q * rows:(q + 1) * rows, h * LANE:(h + 1) * LANE] for q in range(4)])
-            for t in range(4):
-                o_ref[4 * h + t, k] = pieces[t].astype(o_ref.dtype)
+        for h in range(NX // 2):
+            pair = halves(*[acc_ref[k, r * rows:(r + 1) * rows, h * LANE:(h + 1) * LANE] for r in range(2)])
+            for t in range(2):
+                o_ref[2 * h + t, k] = pair[t].astype(o_ref.dtype)
         return carry
 
     lax.fori_loop(0, CLUSTERS, put, 0, unroll=2)
@@ -217,27 +205,39 @@
         compiler_params=SMALL,
         in_specs=[SMEM, SMEM, SMEM, VMEM, VMEM, VMEM],
         out_specs=VMEM,
-        out_shape=jax.ShapeDtypeStruct((NX * NC, CLUSTERS, BLOCK // 4, LANE), jnp.bfloat16),
+        out_shape=jax.ShapeDtypeStruct((NX, CLUSTERS, BLOCK // 2, LANE), jnp.bfloat16),
         scratch_shapes=[pltpu.VMEM((CLUSTERS, BLOCK, COLS), jnp.float32)],
     )(cluster_ids, weight, core, own, got, columns)
 
 
-def final_kernel(m_ref, o_ref):
-    for zb in range(NZB):
-        for a in range(4):
-            pieces = quarters([m_ref[0, b % 2, a, zb, b // 2] for b in range(4)])
-            o_ref[0, zb * BLOCK:(zb + 1) * BLOCK, a * LANE:(a + 1) * LANE] = jnp.concatenate(pieces, 0)
+def final_kernel(m_ref, o_ref, buf_ref, sem):
+    rows = NZB * BLOCK
+
+    def put(x):
+        return pltpu.make_async_copy(buf_ref.at[x % 2], o_ref.at[0, pl.ds(x * rows, rows)], sem.at[x % 2])
+
+    for x in range(NX):
+        if x >= 2:
+            put(x - 2).wait()
+        for zb in range(NZB):
+            for y in range(NY):
+                pair = halves(m_ref[x, y, zb, 0], m_ref[x, y, zb, 1])
+                buf_ref[x % 2, zb * BLOCK:(zb + 1) * BLOCK, y * LANE:(y + 1) * LANE] = jnp.concatenate(pair, 0)
+        put(x).start()
+    for x in range(NX - 2, NX):
+        put(x).wait()
 
 
 def final(merged):
     rows = NZB * BLOCK
+    width = NC * COLS
     return pl.pallas_call(
         final_kernel,
         compiler_params=SMALL,
-        grid=(NX,),
-        in_specs=[pl.BlockSpec((1,) + merged.shape[1:], lambda x: (x,) + (0,) * 6)],
-        out_specs=pl.BlockSpec((1, rows, NC * COLS), lambda x: (0, x, 0)),
-        out_shape=jax.ShapeDtypeStruct((1, NX * rows, NC * COLS), merged.dtype),
+        in_specs=[VMEM],
+        out_specs=ANY,
+        out_shape=jax.ShapeDtypeStruct((1, NX * rows, width), merged.dtype),
+        scratch_shapes=[pltpu.VMEM((2, rows, width), merged.dtype), pltpu.SemaphoreType.DMA((2,))],
     )(merged)
 
 
@@ -258,21 +258,21 @@
     weight = counts.astype(jnp.float32) / jnp.sum(jnp.where(member, total[:, None], 0.0), axis=0)
     core = lax.axis_index("core").astype(jnp.int32).reshape(1)
 
-    held, send = spread(core, w_up)
-    rows = join(core, lax.ppermute(send, "core", SWAP), held)
+    got = lax.ppermute(spread(core, w_up, True), "core", SWAP)
+    rows = join(core, got, spread(core, w_up, False))
     rows = rows.reshape(NZB * SLICES, -1, COLS)
     rows, anchor_of, weight = lax.optimization_barrier((rows, anchor_of, weight))
     columns = exchange(rows, ("zb", "y", "zc")).reshape(EXPERTS, BLOCK, COLS)
 
     got = lax.ppermute(grams(anchor_of, core, columns, True), "core", SWAP)
-    partial = grams(anchor_of, core, columns, False) + got
-    parts = exchange(partial, ("y", "zc"))
+    partial = ((grams(anchor_of, core, columns, False) + got) * SCALE).astype(jnp.float16)
+    parts = exchange(partial, ("y", "zc")).astype(jnp.float32)
     copies = polars(parts.reshape(SLICES, MINE, BLOCK, LANES))
     own = exchange(copies, ("y", "zc")).reshape(GROUPS, BLOCK, LANES)
     merged = align(cluster_ids, weight, core, own, lax.ppermute(own, "core", SWAP), columns)
 
-    merged = exchange(merged.reshape(-1, BLOCK // 4, LANE), ("x", "core", "y", "zb", "zc"))
-    return final(merged.reshape(NX, NC, NY, NZB, NZC, BLOCK // 4, LANE))
+    merged = exchange(merged.reshape(-1, BLOCK // 2, LANE), ("x", "y", "zb", "zc"))
+    return final(merged.reshape(NX, NY, NZB, NZC, BLOCK // 2, LANE))
 
 
 def solution(mesh):

time: 300 us -> 278 us (0.927)
  blocking collectives: 251 us -> 238 us
  Pallas kernels: 28.5 us -> 20.3 us
    all_to_all x4, blocking collectives: 251 us -> 238 us  [exchange(): return lax.all_to_all(value, axes, split_axis=0, concat_axis=0, tiled=True)]
    pallas_call x2 -> x3, Pallas kernels: 11.5 us -> 4.49 us  [the longest x2 2.48 us: spread(): pl.pallas_call(kernel, compiler_params=SMALL, in_specs=[SMEM, VMEM], out_...]
where the time goes in v4:
time: 278 us; the launch traced here: 277 us
  blocking collectives  238 us (86%)
  Pallas kernels  20.3 us (7%)
  waiting for transfers between devices  8.03 us (3%)
  starting transfers between devices  7.12 us (3%)
  local copies, waits for them, and re-layouts  2.8 us (1%)
    all_to_all x4, blocking collectives, exchange(): return lax.all_to_all(value, axes, split_axis=0, concat_axis=0, tiled=True)  238 us
    pallas_call x1, Pallas kernels, polars(): pl.pallas_call(polar_kernel, compiler_params=SMALL, in_specs=[VMEM], out_...  6.05 us
  transfers between devices with their start and end apart: 3, of which 3 were waited for; matrix products, arithmetic and copies ran while one was open for 0% of the time, Pallas kernels for 1%

profile of v4, /device:TPU:1, one launch (start us, length us, event | category | flops | bytes accessed | tf_op | source)
XLA Modules:
  0.0 277.3 jit_solution(2022554279206651299)
XLA Ops:
  0.0 2.8 %copy-done = bf16[4,192,4096]{2,1,0:T(8,128)(2,1)S(1)} copy-done((bf16[4,192,4096]{2,1,0:T(8,128)(2,1)S(1)}, bf16[4,192,4096]{2,1,0:T(8,128)(2,1)}, u32[]{:S(2)}) %copy-start) | copy-done | bytes 6291480
  2.8 1.2 shard_map.37
  4.1 3.3 %collective-permute-start = (bf16[2,8,4,96,256]{4,3,2,1,0:T(8,128)(2,1)S(1)}, bf16[2,8,4,96,256]{4,3,2,1,0:T(8,128)(2,1)S(1)}, u32[]{:S(2)}, u32[]{:S(2)}) collective-permute-start(bf16[2,8,4,96,256]{4,3,2,1,0:T(8,128)(2,1)S(1)} %shard_map.37), channel_id=1, source_target_pairs={{0,1},{1,0},{2,3},{3,2},{4,5},{5,4},{6,7},{7,6},{8,9},{9,8},{10,11... | collective-permute-start | bytes 9437192 | tf_op jit(solution)/shard_map/ppermute | solution.py:261
  7.3 1.2 shard_map.38.held_ref
  8.6 0.1 select_reduce_fusion.3
  8.7 0.1 select_reduce_fusion.1
  8.9 0.1 select_reduce_fusion
  9.0 3.7 %collective-permute-done.got_ref = bf16[2,8,4,96,256]{4,3,2,1,0:T(8,128)(2,1)S(1)} collective-permute-done((bf16[2,8,4,96,256]{4,3,2,1,0:T(8,128)(2,1)S(1)}, bf16[2,8,4,96,256]{4,3,2,1,0:T(8,128)(2,1)S(1)}, u32[]{:S(2)}, u32[]{:S(2)}) %collective-permute-start) | collective-permute-done | bytes 3145760 | tf_op jit(solution)/shard_map/ppermute | solution.py:261
  12.6 0.2 shard_map.39
  12.9 148.8 %all_to_all.20 = bf16[32,384,256]{2,1,0:T(8,128)(2,1)S(1)} all-to-all(bf16[32,384,256]{2,1,0:T(8,128)(2,1)S(1)} %bitcast.12), channel_id=1, replica_groups=mesh['y'=4,'zb'=4,'zc'=2,'x'=4,'core'=2] {'zb','y','zc'}, dimensions={0} | all-to-all | bytes 12582912 | tf_op jit(solution)/shard_map/all_to_all | solution.py:245
  161.7 2.3 shard_map.41
  163.9 1.4 collective-permute-start.1
  165.3 2.3 shard_map.40
  167.6 1.9 collective-permute-done.1
  169.5 0.5 multiply_convert_fusion
  170.0 20.9 %all_to_all.21 = f16[16,96,384]{2,1,0:T(8,128)(2,1)S(1)} all-to-all(f16[16,96,384]{2,1,0:T(8,128)(2,1)S(1)} %multiply_convert_fusion), channel_id=1, replica_groups=mesh['y'=4,'zb'=4,'zc'=2,'x'=4,'core'=2] {'y','zc'}, dimensions={0} | all-to-all | bytes 2359296 | tf_op jit(solution)/shard_map/all_to_all | solution.py:245
  190.9 0.2 convert.1.part_ref
  191.1 6.1 %shard_map.42 = bf16[8,2,96,384]{3,2,1,0:T(8,128)(2,1)S(1)} custom-call(f32[8,2,96,384]{3,2,1,0:T(8,128)S(1)} %convert.1.part_ref), custom_call_target="tpu_custom_call" | custom-call | tf_op jit(solution)/shard_map/pallas_call | solution.py:162
  197.2 18.6 %all_to_all.22 = bf16[8,2,96,384]{3,2,1,0:T(8,128)(2,1)S(1)} all-to-all(bf16[8,2,96,384]{3,2,1,0:T(8,128)(2,1)S(1)} %shard_map.42), channel_id=1, replica_groups=mesh['y'=4,'zb'=4,'zc'=2,'x'=4,'core'=2] {'y','zc'}, dimensions={0} | all-to-all | bytes 2359296 | tf_op jit(solution)/shard_map/all_to_all | solution.py:245
  215.8 2.4 collective-permute-start.2
  218.2 2.5 collective-permute-done.2.got_ref
  220.7 5.1 %shard_map.43 = bf16[4,32,48,128]{3,2,1,0:T(8,128)(2,1)S(1)} custom-call(s32[128]{0:T(128)S(1)} %bitcast.20, f32[128]{0:T(128)S(1)} %convert_divide_fusion.weight_ref, s32[1]{0:T(128)} %bitcast.1.core_ref, bf16[16,96,384]{2,1,0:T(8,128)(2,1)S(1)} %bitcast.16, bf16[16,96,384]{2,1,0:T(8,128)(2,1)S(1)} %collective-permute-done.2.got_ref, ...), custom_call_target="tpu_custom_call" | custom-call | tf_op jit(solution)/shard_map/pallas_call | solution.py:203
  225.8 49.5 %all_to_all.23 = bf16[128,48,128]{2,1,0:T(8,128)(2,1)S(1)} all-to-all(bf16[128,48,128]{2,1,0:T(8,128)(2,1)S(1)} %bitcast.14), channel_id=1, replica_groups=mesh['y'=4,'zb'=4,'zc'=2,'x'=4,'core'=2] {'x','y','zb','zc'}, dimensions={0} | all-to-all | bytes 3145728 | tf_op jit(solution)/shard_map/all_to_all | solution.py:245
  275.3 2.0 shard_map.44
  (9 shorter events, 0.0 us)
Async XLA Ops:
  0.0 2.8 %copy-start = (bf16[4,192,4096]{2,1,0:T(8,128)(2,1)S(1)}, bf16[4,192,4096]{2,1,0:T(8,128)(2,1)}, u32[]{:S(2)}) copy-start(bf16[4,192,4096]{2,1,0:T(8,128)(2,1)} %w_ref.3) | copy-start | bytes 18874372
  4.0 4.5 %copy-start.2 = (s32[128]{0:T(128)S(1)}, s32[128]{0:T(128)}, u32[]{:S(2)}) copy-start(s32[128]{0:T(128)} %param.5) | copy-start | bytes 1540
  4.0 4.6 %copy-start.1 = (s32[128,1]{0,1:T(1,128)S(1)}, s32[128,1]{0,1:T(1,128)}, u32[]{:S(2)}) copy-start(s32[128,1]{0,1:T(1,128)} %param.4) | copy-start | bytes 1540
  4.1 8.6 %collective-permute-start = (bf16[2,8,4,96,256]{4,3,2,1,0:T(8,128)(2,1)S(1)}, bf16[2,8,4,96,256]{4,3,2,1,0:T(8,128)(2,1)S(1)}, u32[]{:S(2)}, u32[]{:S(2)}) collective-permute-start(bf16[2,8,4,96,256]{4,3,2,1,0:T(8,128)(2,1)S(1)} %shard_map.37), channel_id=1, source_target_pairs={{0,1},{1,0},{2,3},{3,2},{4,5},{5,4},{6,7},{7,6},{8,9},{9,8},{10,11... | collective-permute-start | bytes 9437192 | tf_op jit(solution)/shard_map/ppermute | solution.py:261
  163.9 5.6 %collective-permute-start.1 = (f32[16,96,384]{2,1,0:T(8,128)S(1)}, f32[16,96,384]{2,1,0:T(8,128)S(1)}, u32[]{:S(2)}, u32[]{:S(2)}) collective-permute-start(f32[16,96,384]{2,1,0:T(8,128)S(1)} %shard_map.41), channel_id=1, source_target_pairs={{0,1},{1,0},{2,3},{3,2},{4,5},{5,4},{6,7},{7,6},{8,9},{9,8},{10,11... | collective-permute-start | bytes 7077896 | tf_op jit(solution)/shard_map/ppermute | solution.py:267
  215.8 4.9 %collective-permute-start.2 = (bf16[16,96,384]{2,1,0:T(8,128)(2,1)S(1)}, bf16[16,96,384]{2,1,0:T(8,128)(2,1)S(1)}, u32[]{:S(2)}, u32[]{:S(2)}) collective-permute-start(bf16[16,96,384]{2,1,0:T(8,128)(2,1)S(1)} %bitcast.15), channel_id=1, source_target_pairs={{0,1},{1,0},{2,3},{3,2},{4,5},{5,4},{6,7},{7,6},{8,9},{9,8},{10,11... | collective-permute-start | bytes 3538952 | tf_op jit(solution)/shard_map/ppermute | solution.py:272

commit v5 on v4

--- a/solution.py
+++ b/solution.py
@@ -16,6 +16,7 @@
 LANES = PACK * BLOCK
 SLICES = NY * NZC
 SCALE = 8192.0
+PIECES = 2
 GROUPS = EXPERTS // PACK // NC
 MINE = GROUPS // SLICES
 SWAP = [(0, 1), (1, 0)]
@@ -23,6 +24,8 @@
 SMEM = pl.BlockSpec(memory_space=pltpu.SMEM)
 ANY = pl.BlockSpec(memory_space=pl.ANY)
 NT = (((1,), (1,)), ((), ()))
+MEDIUM = pltpu.CompilerParams(vmem_limit_bytes=46 * 2**20)
+LARGE = pltpu.CompilerParams(vmem_limit_bytes=58 * 2**20)
 SMALL = pltpu.CompilerParams(vmem_limit_bytes=20 * 2**20)
 
 
@@ -38,51 +41,70 @@
     )
 
 
-def spread(core, w, other):
+def spread(core, w, other, first, count):
     experts, units, width = w.shape
     blocks = units // BLOCK
     span = width // NX
-
-    def kernel(core_ref, w_ref, o_ref):
+    wide = span // NC
+
+    def kernel(core_ref, w_ref, o_ref, buf_ref, sem):
         half = 1 - core_ref[0] if other else core_ref[0]
         base = 0 if other else half * blocks
-        for e in range(experts):
-            for j in range(blocks):
-                rows = slice(j * BLOCK, (j + 1) * BLOCK)
-                for h in range(NX // 2):
+        start = pl.multiple_of(half * wide, wide)
+
+        def fetch(e, x):
+            source = w_ref.at[first + e, :, pl.ds(x * span + start, wide)]
+            return pltpu.make_async_copy(source, buf_ref.at[e, x], sem.at[e, x])
+
+        for e in range(count):
+            for x in range(NX):
+                fetch(e, x).start()
+        for e in range(count):
+            for h in range(NX // 2):
+                for t in range(2):
+                    fetch(e, 2 * h + t).wait()
+                for j in range(blocks):
+                    rows = slice(j * BLOCK, (j + 1) * BLOCK)
                     for a in range(SLICES // 2):
-                        starts = [(2 * h + t) * span + half * (span // NC) + a * LANE for t in range(2)]
-                        pair = halves(*[w_ref[e, rows, pl.ds(pl.multiple_of(s, LANE), LANE)] for s in starts])
+                        lanes = slice(a * LANE, (a + 1) * LANE)
+                        pair = halves(*[buf_ref[e, 2 * h + t, rows, lanes] for t in range(2)])
                         for b in range(2):
                             o_ref[base + j, 2 * a + b, e, :, h * LANE:(h + 1) * LANE] = pair[b]
 
-    shape = (blocks if other else NC * blocks, SLICES, experts, BLOCK, COLS)
+    shape = (blocks if other else NC * blocks, SLICES, count, BLOCK, COLS)
     return pl.pallas_call(
         kernel,
-        compiler_params=SMALL,
-        in_specs=[SMEM, VMEM],
+        compiler_params=LARGE if other else MEDIUM,
+        in_specs=[SMEM, pl.BlockSpec(memory_space=pltpu.HBM)],
         out_specs=VMEM,
         out_shape=jax.ShapeDtypeStruct(shape, w.dtype),
+        scratch_shapes=[pltpu.VMEM((count, NX, units, wide), w.dtype), pltpu.SemaphoreType.DMA((count, NX))],
     )(core, w)
 
 
-def join_kernel(core_ref, got_ref, held_ref, o_ref, sem):
-    blocks = got_ref.shape[0]
-    copy = pltpu.make_async_copy(got_ref, o_ref.at[pl.ds((1 - core_ref[0]) * blocks, blocks)], sem)
-    copy.start()
-    copy.wait()
+def join_kernel(core_ref, *refs):
+    got_refs, (_, o_ref, sem) = refs[:PIECES], refs[PIECES:]
+    blocks, _, count = got_refs[0].shape[:3]
+    copies = []
+    for k, got_ref in enumerate(got_refs):
+        target = o_ref.at[pl.ds((1 - core_ref[0]) * blocks, blocks), :, pl.ds(k * count, count)]
+        copies.append(pltpu.make_async_copy(got_ref, target, sem.at[k]))
+    for copy in copies:
+        copy.start()
+    for copy in copies:
+        copy.wait()
 
 
 def join(core, got, held):
     return pl.pallas_call(
         join_kernel,
         compiler_params=SMALL,
-        in_specs=[SMEM, ANY, ANY],
+        in_specs=[SMEM] + [ANY] * (PIECES + 1),
         out_specs=ANY,
         out_shape=jax.ShapeDtypeStruct(held.shape, held.dtype),
-        scratch_shapes=[pltpu.SemaphoreType.DMA],
-        input_output_aliases={2: 0},
-    )(core, got, held)
+        scratch_shapes=[pltpu.SemaphoreType.DMA((PIECES,))],
+        input_output_aliases={1 + PIECES: 0},
+    )(core, *got, held)
 
 
 def grams(anchor_of, core, columns, other):
@@ -169,24 +191,40 @@
     )(parts)
 
 
-def align_kernel(cluster_ref, weight_ref, core_ref, own_ref, got_ref, w_ref, o_ref, acc_ref):
+def turn(cluster_ref, weight_ref, polar_ref, w_ref, acc_ref, half):
+    def step(g, carry):
+        packed = polar_ref[g]
+        turned = []
+        for i in range(PACK):
+            p = (half * GROUPS + g) * PACK + i
+            part = jnp.dot(packed[:, i * BLOCK:(i + 1) * BLOCK], w_ref[p], preferred_element_type=jnp.float32)
+            turned.append((part * weight_ref[flip(p)]).astype(jnp.bfloat16).astype(jnp.float32))
+        for i in range(PACK):
+            k = cluster_ref[flip((half * GROUPS + g) * PACK + i)]
+            acc_ref[k] = acc_ref[k] + turned[i]
+        return carry
+
+    lax.fori_loop(0, GROUPS, step, 0, unroll=8)
+
+
+def align_own_kernel(cluster_ref, weight_ref, core_ref, own_ref, w_ref, acc_ref):
     acc_ref[...] = jnp.zeros_like(acc_ref)
-    core = core_ref[0]
-
-    def step(g, carry):
-        for half, ref in ((core, own_ref), (1 - core, got_ref)):
-            packed = ref[g]
-            turned = []
-            for i in range(PACK):
-                p = (half * GROUPS + g) * PACK + i
-                part = jnp.dot(packed[:, i * BLOCK:(i + 1) * BLOCK], w_ref[p], preferred_element_type=jnp.float32)
-                turned.append((part * weight_ref[flip(p)]).astype(jnp.bfloat16).astype(jnp.float32))
-            for i in range(PACK):
-                k = cluster_ref[flip((half * GROUPS + g) * PACK + i)]
-                acc_ref[k] = acc_ref[k] + turned[i]
-        return carry
-
-    lax.fori_loop(0, GROUPS, step, 0, unroll=4)
+    turn(cluster_ref, weight_ref, own_ref, w_ref, acc_ref, core_ref[0])
+
+
+def align_own(cluster_ids, weight, core, own, columns):
+    return pl.pallas_call(
+        align_own_kernel,
+        compiler_params=SMALL,
+        in_specs=[SMEM, SMEM, SMEM, VMEM, VMEM],
+        out_specs=VMEM,
+        out_shape=jax.ShapeDtypeStruct((CLUSTERS, BLOCK, COLS), jnp.float32),
+    )(cluster_ids, weight, core, own, columns)
+
+
+def align_got_kernel(cluster_ref, weight_ref, core_ref, got_ref, w_ref, sum_ref, o_ref, acc_ref):
+    acc_ref[...] = sum_ref[...]
+    turn(cluster_ref, weight_ref, got_ref, w_ref, acc_ref, 1 - core_ref[0])
     rows = BLOCK // 2
 
     def put(k, carry):
@@ -199,15 +237,15 @@
     lax.fori_loop(0, CLUSTERS, put, 0, unroll=2)
 
 
-def align(cluster_ids, weight, core, own, got, columns):
-    return pl.pallas_call(
-        align_kernel,
+def align_got(cluster_ids, weight, core, got, columns, sums):
+    return pl.pallas_call(
+        align_got_kernel,
         compiler_params=SMALL,
         in_specs=[SMEM, SMEM, SMEM, VMEM, VMEM, VMEM],
         out_specs=VMEM,
         out_shape=jax.ShapeDtypeStruct((NX, CLUSTERS, BLOCK // 2, LANE), jnp.bfloat16),
         scratch_shapes=[pltpu.VMEM((CLUSTERS, BLOCK, COLS), jnp.float32)],
-    )(cluster_ids, weight, core, own, got, columns)
+    )(cluster_ids, weight, core, got, columns, sums)
 
 
 def final_kernel(m_ref, o_ref, buf_ref, sem):
@@ -258,8 +296,11 @@
     weight = counts.astype(jnp.float32) / jnp.sum(jnp.where(member, total[:, None], 0.0), axis=0)
     core = lax.axis_index("core").astype(jnp.int32).reshape(1)
 
-    got = lax.ppermute(spread(core, w_up, True), "core", SWAP)
-    rows = join(core, got, spread(core, w_up, False))
+    experts = w_up.shape[0]
+    count = experts // PIECES
+    sent = [spread(core, w_up, True, k * count, count) for k in range(PIECES)]
+    got = [lax.ppermute(piece, "core", SWAP) for piece in sent]
+    rows = join(core, got, spread(core, w_up, False, 0, experts))
     rows = rows.reshape(NZB * SLICES, -1, COLS)
     rows, anchor_of, weight = lax.optimization_barrier((rows, anchor_of, weight))
     columns = exchange(rows, ("zb", "y", "zc")).reshape(EXPERTS, BLOCK, COLS)
@@ -269,7 +310,8 @@
     parts = exchange(partial, ("y", "zc")).astype(jnp.float32)
     copies = polars(parts.reshape(SLICES, MINE, BLOCK, LANES))
     own = exchange(copies, ("y", "zc")).reshape(GROUPS, BLOCK, LANES)
-    merged = align(cluster_ids, weight, core, own, lax.ppermute(own, "core", SWAP), columns)
+    got = lax.ppermute(own, "core", SWAP)
+    merged = align_got(cluster_ids, weight, core, got, columns, align_own(cluster_ids, weight, core, own, columns))
 
     merged = exchange(merged.reshape(-1, BLOCK // 2, LANE), ("x", "y", "zb", "zc"))
     return final(merged.reshape(NX, NY, NZB, NZC, BLOCK // 2, LANE))

time: 278 us -> 276 us (level)
  Pallas kernels: 20.3 us -> 27.1 us
  waiting for transfers between devices: 8.03 us -> 2.88 us
  local copies, waits for them, and re-layouts: 2.8 us -> 0.01 us
    pallas_call x4 -> x6, Pallas kernels: 7.75 us -> 14.5 us  [the longest x3 8.47 us: spread(): pl.pallas_call(kernel, compiler_params=LARGE if other else MEDIUM, in_spe...]
    ppermute x2 -> x3, waiting for transfers between devices: 6.13 us -> 0.98 us  [the longest x2 0.64 us: on_device(): got = [lax.ppermute(piece, 'core', SWAP) for piece in sent]]
    unnamed x6 -> x4, local copies, waits for them, and re-layouts: 2.8 us -> 0.01 us
    ppermute x2 -> x3, starting transfers between devices: 5.71 us -> 5.82 us  [the longest x2 3.4 us: on_device(): got = [lax.ppermute(piece, 'core', SWAP) for piece in sent]]
  transfers between devices with their start and end apart: 3 -> 4, of which waited for: 3 -> 3; matrix products, arithmetic and copies ran while one was open for 0% -> 0% of each run, Pallas kernels for 1% -> 4%
where the time goes in v5:
time: 276 us
  blocking collectives  238 us (86%)
  Pallas kernels  27.1 us (10%)
  starting transfers between devices  7.03 us (3%)
  waiting for transfers between devices  2.88 us (1%)
    all_to_all x4, blocking collectives, exchange(): return lax.all_to_all(value, axes, split_axis=0, concat_axis=0, tiled=True)  238 us
    pallas_call x3, Pallas kernels, spread(): pl.pallas_call(kernel, compiler_params=LARGE if other else MEDIUM, in_spe...  8.47 us
    pallas_call x1, Pallas kernels, polars(): pl.pallas_call(polar_kernel, compiler_params=SMALL, in_specs=[VMEM], out_...  6.05 us
  transfers between devices with their start and end apart: 4, of which 3 were waited for; matrix products, arithmetic and copies ran while one was open for 0% of the time, Pallas kernels for 4%

profile of v5, /device:TPU:1, one launch (start us, length us, event | category | flops | bytes accessed | tf_op | source)
XLA Modules:
  0.0 276.2 jit_solution(9572062780329763590)
XLA Ops:
  0.0 2.9 %shard_map.37 = bf16[2,8,2,96,256]{4,3,2,1,0:T(8,128)(2,1)} custom-call(s32[1]{0:T(128)} %bitcast.1.core_ref, bf16[4,192,4096]{2,1,0:T(8,128)(2,1)} %w_ref.5), custom_call_target="tpu_custom_call" | custom-call | tf_op jit(solution)/shard_map/pallas_call | solution.py:75
  3.0 3.3 %collective-permute-start = (bf16[2,8,2,96,256]{4,3,2,1,0:T(8,128)(2,1)}, bf16[2,8,2,96,256]{4,3,2,1,0:T(8,128)(2,1)S(1)}, u32[]{:S(2)}, u32[]{:S(2)}) collective-permute-start(bf16[2,8,2,96,256]{4,3,2,1,0:T(8,128)(2,1)} %shard_map.37), channel_id=1, source_target_pairs={{0,1},{1,0},{2,3},{3,2},{4,5},{5,4},{6,7},{7,6},{8,9},{9,8},{10,11... | collective-permute-start | bytes 4718600 | tf_op jit(solution)/shard_map/ppermute | solution.py:302
  6.2 3.0 %shard_map.38 = bf16[2,8,2,96,256]{4,3,2,1,0:T(8,128)(2,1)} custom-call(s32[1]{0:T(128)} %bitcast.1.core_ref, bf16[4,192,4096]{2,1,0:T(8,128)(2,1)} %w_ref.5), custom_call_target="tpu_custom_call" | custom-call | tf_op jit(solution)/shard_map/pallas_call | solution.py:75
  9.3 2.6 shard_map.39.refs_2_
  11.9 0.1 select_reduce_fusion.3
  12.1 0.1 select_reduce_fusion.1
  12.3 0.6 collective-permute-done.1.refs_1_
  12.9 0.2 shard_map.40
  13.2 148.8 %all_to_all.20 = bf16[32,384,256]{2,1,0:T(8,128)(2,1)S(1)} all-to-all(bf16[32,384,256]{2,1,0:T(8,128)(2,1)S(1)} %bitcast.13), channel_id=1, replica_groups=mesh['y'=4,'zb'=4,'zc'=2,'x'=4,'core'=2] {'zb','y','zc'}, dimensions={0} | all-to-all | bytes 12582912 | tf_op jit(solution)/shard_map/all_to_all | solution.py:283
  161.9 2.3 shard_map.42
  164.2 1.2 collective-permute-start.2
  165.4 2.3 shard_map.41
  167.7 1.9 collective-permute-done.2
  169.6 0.4 multiply_convert_fusion
  170.0 21.1 %all_to_all.21 = f16[16,96,384]{2,1,0:T(8,128)(2,1)S(1)} all-to-all(f16[16,96,384]{2,1,0:T(8,128)(2,1)S(1)} %multiply_convert_fusion), channel_id=1, replica_groups=mesh['y'=4,'zb'=4,'zc'=2,'x'=4,'core'=2] {'y','zc'}, dimensions={0} | all-to-all | bytes 2359296 | tf_op jit(solution)/shard_map/all_to_all | solution.py:283
  191.1 0.2 convert.1.part_ref
  191.4 6.0 %shard_map.43 = bf16[8,2,96,384]{3,2,1,0:T(8,128)(2,1)S(1)} custom-call(f32[8,2,96,384]{3,2,1,0:T(8,128)S(1)} %convert.1.part_ref), custom_call_target="tpu_custom_call" | custom-call | tf_op jit(solution)/shard_map/pallas_call | solution.py:184
  197.4 18.6 %all_to_all.22 = bf16[8,2,96,384]{3,2,1,0:T(8,128)(2,1)S(1)} all-to-all(bf16[8,2,96,384]{3,2,1,0:T(8,128)(2,1)S(1)} %shard_map.43), channel_id=1, replica_groups=mesh['y'=4,'zb'=4,'zc'=2,'x'=4,'core'=2] {'y','zc'}, dimensions={0} | all-to-all | bytes 2359296 | tf_op jit(solution)/shard_map/all_to_all | solution.py:283
  216.1 2.4 collective-permute-start.3
  218.5 2.1 shard_map.44.sum_ref
  220.6 0.3 collective-permute-done.3.got_ref
  221.0 3.7 %shard_map.45 = bf16[4,32,48,128]{3,2,1,0:T(8,128)(2,1)S(1)} custom-call(s32[128]{0:T(128)S(1)} %bitcast.22, f32[128]{0:T(128)S(1)} %convert_divide_fusion.weight_ref, s32[1]{0:T(128)} %bitcast.1.core_ref, bf16[16,96,384]{2,1,0:T(8,128)(2,1)S(1)} %collective-permute-done.3.got_ref, bf16[128,96,256]{2,1,0:T(8,128)(2,1)S(1)} %bitcast.12, ...), custom_call_target="tpu_custom_call" | custom-call | tf_op jit(solution)/shard_map/pallas_call | solution.py:241
  224.7 49.5 %all_to_all.23 = bf16[128,48,128]{2,1,0:T(8,128)(2,1)S(1)} all-to-all(bf16[128,48,128]{2,1,0:T(8,128)(2,1)S(1)} %bitcast.14), channel_id=1, replica_groups=mesh['y'=4,'zb'=4,'zc'=2,'x'=4,'core'=2] {'x','y','zb','zc'}, dimensions={0} | all-to-all | bytes 3145728 | tf_op jit(solution)/shard_map/all_to_all | solution.py:283
  274.2 2.0 shard_map.46
  (11 shorter events, 0.2 us)
Async XLA Ops:
  3.0 9.3 %collective-permute-start = (bf16[2,8,2,96,256]{4,3,2,1,0:T(8,128)(2,1)}, bf16[2,8,2,96,256]{4,3,2,1,0:T(8,128)(2,1)S(1)}, u32[]{:S(2)}, u32[]{:S(2)}) collective-permute-start(bf16[2,8,2,96,256]{4,3,2,1,0:T(8,128)(2,1)} %shard_map.37), channel_id=1, source_target_pairs={{0,1},{1,0},{2,3},{3,2},{4,5},{5,4},{6,7},{7,6},{8,9},{9,8},{10,11... | collective-permute-start | bytes 4718600 | tf_op jit(solution)/shard_map/ppermute | solution.py:302
  9.2 2.7 copy-start.1
  9.2 2.7 copy-start
  9.2 3.7 %collective-permute-start.1 = (bf16[2,8,2,96,256]{4,3,2,1,0:T(8,128)(2,1)}, bf16[2,8,2,96,256]{4,3,2,1,0:T(8,128)(2,1)S(1)}, u32[]{:S(2)}, u32[]{:S(2)}) collective-permute-start(bf16[2,8,2,96,256]{4,3,2,1,0:T(8,128)(2,1)} %shard_map.38), channel_id=1, source_target_pairs={{0,1},{1,0},{2,3},{3,2},{4,5},{5,4},{6,7},{7,6},{8,9},{9,8},{10,11... | collective-permute-start | bytes 4718600 | tf_op jit(solution)/shard_map/ppermute | solution.py:302
  164.2 5.4 %collective-permute-start.2 = (f32[16,96,384]{2,1,0:T(8,128)S(1)}, f32[16,96,384]{2,1,0:T(8,128)S(1)}, u32[]{:S(2)}, u32[]{:S(2)}) collective-permute-start(f32[16,96,384]{2,1,0:T(8,128)S(1)} %shard_map.42), channel_id=1, source_target_pairs={{0,1},{1,0},{2,3},{3,2},{4,5},{5,4},{6,7},{7,6},{8,9},{9,8},{10,11... | collective-permute-start | bytes 7077896 | tf_op jit(solution)/shard_map/ppermute | solution.py:308
  216.1 4.9 %collective-permute-start.3 = (bf16[16,96,384]{2,1,0:T(8,128)(2,1)S(1)}, bf16[16,96,384]{2,1,0:T(8,128)(2,1)S(1)}, u32[]{:S(2)}, u32[]{:S(2)}) collective-permute-start(bf16[16,96,384]{2,1,0:T(8,128)(2,1)S(1)} %bitcast.16), channel_id=1, source_target_pairs={{0,1},{1,0},{2,3},{3,2},{4,5},{5,4},{6,7},{7,6},{8,9},{9,8},{10,11... | collective-permute-start | bytes 3538952 | tf_op jit(solution)/shard_map/ppermute | solution.py:313

commit v6 on v4

--- a/solution.py
+++ b/solution.py
@@ -1,9 +1,12 @@
+import functools
+
 import jax
 import jax.numpy as jnp
 from jax import lax
 from jax.experimental import pallas as pl
 from jax.experimental.pallas import tpu as pltpu
 from jax.sharding import Mesh, PartitionSpec as P
+
 
 BLOCK = 96
 NS_STEPS = 8
@@ -16,6 +19,8 @@
 LANES = PACK * BLOCK
 SLICES = NY * NZC
 SCALE = 8192.0
+PARTS = 2
+ROWS = BLOCK // PARTS
 GROUPS = EXPERTS // PACK // NC
 MINE = GROUPS // SLICES
 SWAP = [(0, 1), (1, 0)]
@@ -118,7 +123,8 @@
     return product[:BLOCK, :LANE] + product[BLOCK:, :LANE] + product[:BLOCK, LANE:]
 
 
-def polar_kernel(part_ref, o_ref, x_ref):
+def polar_kernel(part_ref, *refs):
+    o_refs, x_ref = refs[:PARTS], refs[PARTS]
     count = MINE * PACK
     for g in range(MINE):
         total = part_ref[0, g]
@@ -153,9 +159,10 @@
 
     lax.fori_loop(0, NS_STEPS, step, 0)
     for g in range(MINE):
-        packed = jnp.concatenate([x_ref[g * PACK + i][:, :BLOCK] for i in range(PACK)], axis=1).astype(o_ref.dtype)
+        packed = jnp.concatenate([x_ref[g * PACK + i][:, :BLOCK] for i in range(PACK)], axis=1).astype(jnp.bfloat16)
         for s in range(SLICES):
-            o_ref[s, g] = packed
+            o_refs[0][s, g] = packed[:ROWS]
+        o_refs[1][g] = packed[ROWS:]
 
 
 def polars(parts):
@@ -163,19 +170,27 @@
         polar_kernel,
         compiler_params=SMALL,
         in_specs=[VMEM],
-        out_specs=VMEM,
-        out_shape=jax.ShapeDtypeStruct((SLICES, MINE, BLOCK, LANES), jnp.bfloat16),
+        out_specs=[VMEM] * PARTS,
+        out_shape=[
+            jax.ShapeDtypeStruct((SLICES, MINE, ROWS, LANES), jnp.bfloat16),
+            jax.ShapeDtypeStruct((MINE, ROWS, LANES), jnp.bfloat16),
+        ],
         scratch_shapes=[pltpu.VMEM((MINE * PACK, BLOCK, LANE), jnp.float32)],
     )(parts)
 
 
-def align_kernel(cluster_ref, weight_ref, core_ref, own_ref, got_ref, w_ref, o_ref, acc_ref):
+def align_kernel(cluster_ref, weight_ref, place_ref, own_ref, got_ref, w_ref, o_ref, acc_ref, *, relative):
     acc_ref[...] = jnp.zeros_like(acc_ref)
-    core = core_ref[0]
+    core = place_ref[0]
 
     def step(g, carry):
+        held = g
+        if relative:
+            source = g // MINE
+            behind = (place_ref[1] + NY - source // NZC) % NY
+            held = (behind * NZC + (place_ref[2] + source) % NZC) * MINE + g % MINE
         for half, ref in ((core, own_ref), (1 - core, got_ref)):
-            packed = ref[g]
+            packed = ref[held]
             turned = []
             for i in range(PACK):
                 p = (half * GROUPS + g) * PACK + i
@@ -187,7 +202,7 @@
         return carry
 
     lax.fori_loop(0, GROUPS, step, 0, unroll=4)
-    rows = BLOCK // 2
+    rows = ROWS // 2
 
     def put(k, carry):
         for h in range(NX // 2):
@@ -199,18 +214,19 @@
     lax.fori_loop(0, CLUSTERS, put, 0, unroll=2)
 
 
-def align(cluster_ids, weight, core, own, got, columns):
-    return pl.pallas_call(
-        align_kernel,
+def align(cluster_ids, weight, place, own, got, columns, relative):
+    return pl.pallas_call(
+        functools.partial(align_kernel, relative=relative),
         compiler_params=SMALL,
         in_specs=[SMEM, SMEM, SMEM, VMEM, VMEM, VMEM],
         out_specs=VMEM,
-        out_shape=jax.ShapeDtypeStruct((NX, CLUSTERS, BLOCK // 2, LANE), jnp.bfloat16),
-        scratch_shapes=[pltpu.VMEM((CLUSTERS, BLOCK, COLS), jnp.float32)],
-    )(cluster_ids, weight, core, own, got, columns)
-
-
-def final_kernel(m_ref, o_ref, buf_ref, sem):
+        out_shape=jax.ShapeDtypeStruct((NX, CLUSTERS, ROWS // 2, LANE), jnp.bfloat16),
+        scratch_shapes=[pltpu.VMEM((CLUSTERS, ROWS, COLS), jnp.float32)],
+    )(cluster_ids, weight, place, own, got, columns)
+
+
+def final_kernel(*refs):
+    m_refs, (o_ref, buf_ref, sem) = refs[:PARTS], refs[PARTS:]
     rows = NZB * BLOCK
 
     def put(x):
@@ -221,24 +237,24 @@
             put(x - 2).wait()
         for zb in range(NZB):
             for y in range(NY):
-                pair = halves(m_ref[x, y, zb, 0], m_ref[x, y, zb, 1])
-                buf_ref[x % 2, zb * BLOCK:(zb + 1) * BLOCK, y * LANE:(y + 1) * LANE] = jnp.concatenate(pair, 0)
+                pieces = [p for m_ref in m_refs for p in halves(m_ref[x, y, zb, 0], m_ref[x, y, zb, 1])]
+                buf_ref[x % 2, zb * BLOCK:(zb + 1) * BLOCK, y * LANE:(y + 1) * LANE] = jnp.concatenate(pieces, 0)
         put(x).start()
     for x in range(NX - 2, NX):
         put(x).wait()
 
 
-def final(merged):
+def final(*merged):
     rows = NZB * BLOCK
     width = NC * COLS
     return pl.pallas_call(
         final_kernel,
         compiler_params=SMALL,
-        in_specs=[VMEM],
+        in_specs=[VMEM] * PARTS,
         out_specs=ANY,
-        out_shape=jax.ShapeDtypeStruct((1, NX * rows, width), merged.dtype),
-        scratch_shapes=[pltpu.VMEM((2, rows, width), merged.dtype), pltpu.SemaphoreType.DMA((2,))],
-    )(merged)
+        out_shape=jax.ShapeDtypeStruct((1, NX * rows, width), jnp.bfloat16),
+        scratch_shapes=[pltpu.VMEM((2, rows, width), jnp.bfloat16), pltpu.SemaphoreType.DMA((2,))],
+    )(*merged)
 
 
 def exchange(value, axes):
@@ -268,11 +284,25 @@
     partial = ((grams(anchor_of, core, columns, False) + got) * SCALE).astype(jnp.float16)
     parts = exchange(partial, ("y", "zc")).astype(jnp.float32)
     copies = polars(parts.reshape(SLICES, MINE, BLOCK, LANES))
-    own = exchange(copies, ("y", "zc")).reshape(GROUPS, BLOCK, LANES)
-    merged = align(cluster_ids, weight, core, own, lax.ppermute(own, "core", SWAP), columns)
-
-    merged = exchange(merged.reshape(-1, BLOCK // 2, LANE), ("x", "y", "zb", "zc"))
-    return final(merged.reshape(NX, NY, NZB, NZC, BLOCK // 2, LANE))
+
+    place = jnp.stack([lax.axis_index(name).astype(jnp.int32) for name in ("core", "y", "zc")])
+
+    def serve(rows):
+        rows = exchange(rows.reshape(-1, ROWS // 2, LANE), ("x", "y", "zb", "zc"))
+        return rows.reshape(NX, NY, NZB, NZC, ROWS // 2, LANE)
+
+    def ahead(dy, dz):
+        return [(y * NZC + z, (y + dy) % NY * NZC + (z + dz) % NZC) for y in range(NY) for z in range(NZC)]
+
+    own = exchange(copies[0], ("y", "zc")).reshape(GROUPS, ROWS, LANES)
+    merged = align(cluster_ids, weight, place, own, lax.ppermute(own, "core", SWAP), columns, False)
+    first = serve(merged)
+    pieces = [copies[1]]
+    for offset in range(1, SLICES):
+        pieces.append(lax.ppermute(copies[1], ("y", "zc"), ahead(offset // NZC, offset % NZC)))
+    own = jnp.concatenate(pieces, axis=0)
+    second = serve(align(cluster_ids, weight, place, own, lax.ppermute(own, "core", SWAP), columns, True))
+    return final(first, second)
 
 
 def solution(mesh):

time: 278 us -> 298 us (1.072)
  blocking collectives: 238 us -> 199 us
  starting transfers between devices: 7.12 us -> 35 us
  waiting for transfers between devices: 8.03 us -> 27.9 us
  local copies, waits for them, and re-layouts: 2.8 us -> 8.49 us
  Pallas kernels: 20.3 us -> 24.8 us
    all_to_all x4 -> x3, blocking collectives: 238 us -> 199 us  [exchange(): return lax.all_to_all(value, axes, split_axis=0, concat_axis=0, tiled=True)]
    all_to_all x0 -> x2, waiting for transfers between devices: none -> 16 us  [exchange(): return lax.all_to_all(value, axes, split_axis=0, concat_axis=0, tiled=True)]
    all_to_all x0 -> x2, starting transfers between devices: none -> 13.7 us  [exchange(): return lax.all_to_all(value, axes, split_axis=0, concat_axis=0, tiled=True)]
    ppermute x0 -> x7, starting transfers between devices: none -> 10.2 us  [on_device(): lax.ppermute(copies[1], ('y', 'zc'), ahead(offset // NZC, offset % NZC))]
    unnamed x6 -> x19, local copies, waits for them, and re-layouts: 2.8 us -> 8.48 us
    ppermute x1 -> x2, starting transfers between devices: 2.43 us -> 6.32 us  [on_device(): lax.ppermute(own, 'core', SWAP)]
    pallas_call x2 -> x3, Pallas kernels: 7.07 us -> 10.8 us  [the longest x2 8.63 us: align(): pl.pallas_call(functools.partial(align_kernel, relative=relative), compil...]
    ppermute x0 -> x7, waiting for transfers between devices: none -> 3.14 us  [on_device(): lax.ppermute(copies[1], ('y', 'zc'), ahead(offset // NZC, offset % NZC))]
  transfers between devices with their start and end apart: 3 -> 13, of which waited for: 3 -> 7; matrix products, arithmetic and copies ran while one was open for 0% -> 0% of each run, Pallas kernels for 1% -> 4%
where the time goes in v6:
time: 298 us; the launch traced here: 296 us
  blocking collectives  199 us (67%)
  starting transfers between devices  35 us (12%)
  waiting for transfers between devices  27.9 us (9%)
  Pallas kernels  24.8 us (8%)
  local copies, waits for them, and re-layouts  8.49 us (3%)
    all_to_all x3, blocking collectives, exchange(): return lax.all_to_all(value, axes, split_axis=0, concat_axis=0, tiled=True)  199 us
    all_to_all x2, waiting for transfers between devices, exchange(): return lax.all_to_all(value, axes, split_axis=0, concat_axis=0, tiled=True)  16 us
    all_to_all x2, starting transfers between devices, exchange(): return lax.all_to_all(value, axes, split_axis=0, concat_axis=0, tiled=True)  13.7 us
    ppermute x7, starting transfers between devices, on_device(): lax.ppermute(copies[1], ('y', 'zc'), ahead(offset // NZC, offset % NZC))  10.2 us
    pallas_call x2, Pallas kernels, align(): pl.pallas_call(functools.partial(align_kernel, relative=relative), compil...  8.63 us
    unnamed x19, local copies, waits for them, and re-layouts  8.48 us
    pallas_call x1, Pallas kernels, polars(): pl.pallas_call(polar_kernel, compiler_params=SMALL, in_specs=[VMEM], out_...  6.84 us
    ppermute x2, starting transfers between devices, on_device(): lax.ppermute(own, 'core', SWAP)  6.32 us
  transfers between devices with their start and end apart: 13, of which 7 were waited for; matrix products, arithmetic and copies ran while one was open for 0% of the time, Pallas kernels for 4%

profile of v6, /device:TPU:1, one launch (start us, length us, event | category | flops | bytes accessed | tf_op | source)
XLA Modules:
  0.0 296.4 jit_solution(2997301659789243982)
XLA Ops:
  0.0 2.8 copy-done.3
  4.1 3.3 %collective-permute-start = (bf16[2,8,4,96,256]{4,3,2,1,0:T(8,128)(2,1)S(1)}, bf16[2,8,4,96,256]{4,3,2,1,0:T(8,128)(2,1)S(1)}, u32[]{:S(2)}, u32[]{:S(2)}) collective-permute-start(bf16[2,8,4,96,256]{4,3,2,1,0:T(8,128)(2,1)S(1)} %shard_map.37), channel_id=1, source_target_pairs={{0,1},{1,0},{2,3},{3,2},{4,5},{5,4},{6,7},{7,6},{8,9},{9,8},{10,11... | collective-permute-start | bytes 9437192 | tf_op jit(solution)/shard_map/ppermute | solution.py:277
  9.0 3.7 %collective-permute-done.got_ref = bf16[2,8,4,96,256]{4,3,2,1,0:T(8,128)(2,1)S(1)} collective-permute-done((bf16[2,8,4,96,256]{4,3,2,1,0:T(8,128)(2,1)S(1)}, bf16[2,8,4,96,256]{4,3,2,1,0:T(8,128)(2,1)S(1)}, u32[]{:S(2)}, u32[]{:S(2)}) %collective-permute-start) | collective-permute-done | bytes 3145760 | tf_op jit(solution)/shard_map/ppermute | solution.py:277
  12.9 148.8 %all_to_all.25 = bf16[32,384,256]{2,1,0:T(8,128)(2,1)S(1)} all-to-all(bf16[32,384,256]{2,1,0:T(8,128)(2,1)S(1)} %bitcast.17), channel_id=1, replica_groups=mesh['y'=4,'zb'=4,'zc'=2,'x'=4,'core'=2] {'zb','y','zc'}, dimensions={0} | all-to-all | bytes 12582912 | tf_op jit(solution)/shard_map/all_to_all | solution.py:261
  161.7 2.3 shard_map.41
  165.3 2.3 shard_map.40
  167.6 1.9 collective-permute-done.1
  170.0 20.9 %all_to_all.26 = f16[16,96,384]{2,1,0:T(8,128)(2,1)S(1)} all-to-all(f16[16,96,384]{2,1,0:T(8,128)(2,1)S(1)} %multiply_convert_fusion), channel_id=1, replica_groups=mesh['y'=4,'zb'=4,'zc'=2,'x'=4,'core'=2] {'y','zc'}, dimensions={0} | all-to-all | bytes 2359296 | tf_op jit(solution)/shard_map/all_to_all | solution.py:261
  191.1 6.8 %shard_map.42 = (bf16[8,2,48,384]{3,2,1,0:T(8,128)(2,1)}, bf16[2,48,384]{2,1,0:T(8,128)(2,1)S(1)}) custom-call(f32[8,2,96,384]{3,2,1,0:T(8,128)S(1)} %convert.1.part_ref), custom_call_target="tpu_custom_call" | custom-call | tf_op jit(solution)/shard_map/pallas_call | solution.py:169
  199.9 3.1 %collective-permute-start.6 = (bf16[2,48,384]{2,1,0:T(8,128)(2,1)S(1)}, bf16[2,48,384]{2,1,0:T(8,128)(2,1)S(1)}, u32[]{:S(2)}, u32[]{:S(2)}) collective-permute-start(bf16[2,48,384]{2,1,0:T(8,128)(2,1)S(1)} %get-tuple-element.14), channel_id=1, source_target_pairs={{0,128},{8,136},{64,192},{72,200},{128,0},{136,8},{192,64},{200,72... | collective-permute-start | bytes 221192 | tf_op jit(solution)/shard_map/ppermute | solution.py:302
  203.9 4.2 %all-to-all-start.2 = ((bf16[8,2,48,384]{3,2,1,0:T(8,128)(2,1)}), bf16[8,2,48,384]{3,2,1,0:T(8,128)(2,1)S(1)}, u32[]{:S(2)}, u32[]{:S(2)}) async-start(bf16[8,2,48,384]{3,2,1,0:T(8,128)(2,1)} %get-tuple-element.13), calls=%async_computation.2 | async-start | bytes 1179648 | tf_op jit(solution)/shard_map/all_to_all | solution.py:261
  208.2 2.8 collective-permute-start.8
  212.6 2.7 collective-permute-done.8
  215.8 5.6 %collective-permute-start.10 = (bf16[16,48,384]{2,1,0:T(8,128)(2,1)S(1)}, bf16[16,48,384]{2,1,0:T(8,128)(2,1)S(1)}, u32[]{:S(2)}, u32[]{:S(2)}) collective-permute-start(bf16[16,48,384]{2,1,0:T(8,128)(2,1)S(1)} %constant_dynamic-update-slice_fusion.own_ref), channel_id=1, source_target_pairs={{0,1},{1,0},{2,3},{3,2},{4,5},{5,4},{6,7},{7,6},{8,9},{9,8},{10,11... | collective-permute-start | bytes 1769480 | tf_op jit(solution)/shard_map/ppermute | solution.py:304
  221.4 1.6 collective-permute-done.10.got_ref
  223.0 2.8 copy-done.1
  225.8 4.8 %shard_map.44 = bf16[4,32,24,128]{3,2,1,0:T(8,128)(2,1)} custom-call(s32[128]{0:T(128)S(1)} %bitcast.26, f32[128]{0:T(128)S(1)} %convert_divide_fusion.weight_ref, s32[3]{0:T(128)S(1)} %pad_add_fusion.place_ref, bf16[16,48,384]{2,1,0:T(8,128)(2,1)S(1)} %constant_dynamic-update-slice_fusion.own_ref, bf16[16,48,384]{2,1,0:T(8,128)(2,1)S(1)} %collective-permute-done.10.got_ref, ...), custom_call_target="tpu_custom_call" | custom-call | tf_op jit(solution)/shard_map/pallas_call | solution.py:218
  230.5 9.4 %all-to-all-start.4 = ((bf16[128,24,128]{2,1,0:T(8,128)(2,1)}), bf16[128,24,128]{2,1,0:T(8,128)(2,1)S(1)}, u32[]{:S(2)}, u32[]{:S(2)}) async-start(bf16[128,24,128]{2,1,0:T(8,128)(2,1)} %bitcast.10), calls=%async_computation.4 | async-start | bytes 1572864 | tf_op jit(solution)/shard_map/all_to_all | solution.py:261
  240.7 1.6 collective-permute-done.2.got_ref
  242.4 2.8 copy-done.2
  245.2 3.8 %shard_map.43 = bf16[4,32,24,128]{3,2,1,0:T(8,128)(2,1)S(1)} custom-call(s32[128]{0:T(128)S(1)} %bitcast.27, f32[128]{0:T(128)S(1)} %convert_divide_fusion.weight_ref, s32[3]{0:T(128)S(1)} %pad_add_fusion.place_ref, bf16[16,48,384]{2,1,0:T(8,128)(2,1)S(1)} %bitcast.22, bf16[16,48,384]{2,1,0:T(8,128)(2,1)S(1)} %collective-permute-done.2.got_ref, ...), custom_call_target="tpu_custom_call" | custom-call | tf_op jit(solution)/shard_map/pallas_call | solution.py:218
  249.0 16.0 %all-to-all-done.4 = bf16[128,24,128]{2,1,0:T(8,128)(2,1)S(1)} async-done(((bf16[128,24,128]{2,1,0:T(8,128)(2,1)}), bf16[128,24,128]{2,1,0:T(8,128)(2,1)S(1)}, u32[]{:S(2)}, u32[]{:S(2)}) %all-to-all-start.4) | async-done | bytes 786464 | tf_op jit(solution)/shard_map/all_to_all | solution.py:261
  265.0 29.1 %all_to_all.27 = bf16[128,24,128]{2,1,0:T(8,128)(2,1)S(1)} all-to-all(bf16[128,24,128]{2,1,0:T(8,128)(2,1)S(1)} %bitcast.18), channel_id=1, replica_groups=mesh['y'=4,'zb'=4,'zc'=2,'x'=4,'core'=2] {'x','y','zb','zc'}, dimensions={0} | all-to-all | bytes 1572864 | tf_op jit(solution)/shard_map/all_to_all | solution.py:261
  294.1 2.1 shard_map.45
  (44 shorter events, 11.0 us)
Async XLA Ops:
  0.0 2.8 copy-start.3
  4.0 4.5 %copy-start.5 = (s32[128]{0:T(128)S(1)}, s32[128]{0:T(128)}, u32[]{:S(2)}) copy-start(s32[128]{0:T(128)} %param.5) | copy-start | bytes 1540
  4.0 4.6 %copy-start.4 = (s32[128,1]{0,1:T(1,128)S(1)}, s32[128,1]{0,1:T(1,128)}, u32[]{:S(2)}) copy-start(s32[128,1]{0,1:T(1,128)} %param.4) | copy-start | bytes 1540
  4.1 8.6 %collective-permute-start = (bf16[2,8,4,96,256]{4,3,2,1,0:T(8,128)(2,1)S(1)}, bf16[2,8,4,96,256]{4,3,2,1,0:T(8,128)(2,1)S(1)}, u32[]{:S(2)}, u32[]{:S(2)}) collective-permute-start(bf16[2,8,4,96,256]{4,3,2,1,0:T(8,128)(2,1)S(1)} %shard_map.37), channel_id=1, source_target_pairs={{0,1},{1,0},{2,3},{3,2},{4,5},{5,4},{6,7},{7,6},{8,9},{9,8},{10,11... | collective-permute-start | bytes 9437192 | tf_op jit(solution)/shard_map/ppermute | solution.py:277
  161.7 3.7 %copy-start = (bf16[32,384,256]{2,1,0:T(8,128)(2,1)}, bf16[32,384,256]{2,1,0:T(8,128)(2,1)S(1)}, u32[]{:S(2)}) copy-start(bf16[32,384,256]{2,1,0:T(8,128)(2,1)S(1)} %all_to_all.25) | copy-start | bytes 18874372
  163.9 5.6 %collective-permute-start.1 = (f32[16,96,384]{2,1,0:T(8,128)S(1)}, f32[16,96,384]{2,1,0:T(8,128)S(1)}, u32[]{:S(2)}, u32[]{:S(2)}) collective-permute-start(f32[16,96,384]{2,1,0:T(8,128)S(1)} %shard_map.41), channel_id=1, source_target_pairs={{0,1},{1,0},{2,3},{3,2},{4,5},{5,4},{6,7},{7,6},{8,9},{9,8},{10,11... | collective-permute-start | bytes 7077896 | tf_op jit(solution)/shard_map/ppermute | solution.py:283
  198.0 10.2 %collective-permute-start.3 = (bf16[2,48,384]{2,1,0:T(8,128)(2,1)S(1)}, bf16[2,48,384]{2,1,0:T(8,128)(2,1)S(1)}, u32[]{:S(2)}, u32[]{:S(2)}) collective-permute-start(bf16[2,48,384]{2,1,0:T(8,128)(2,1)S(1)} %get-tuple-element.14), channel_id=1, source_target_pairs={{0,8},{8,0},{64,72},{72,64},{128,136},{136,128},{192,200},{200,192... | collective-permute-start | bytes 221192 | tf_op jit(solution)/shard_map/ppermute | solution.py:302
  199.1 11.8 %collective-permute-start.4 = (bf16[2,48,384]{2,1,0:T(8,128)(2,1)S(1)}, bf16[2,48,384]{2,1,0:T(8,128)(2,1)S(1)}, u32[]{:S(2)}, u32[]{:S(2)}) collective-permute-start(bf16[2,48,384]{2,1,0:T(8,128)(2,1)S(1)} %get-tuple-element.14), channel_id=1, source_target_pairs={{0,64},{8,72},{64,128},{72,136},{128,192},{136,200},{192,0},{200,8... | collective-permute-start | bytes 221192 | tf_op jit(solution)/shard_map/ppermute | solution.py:302
  199.4 13.1 %collective-permute-start.5 = (bf16[2,48,384]{2,1,0:T(8,128)(2,1)S(1)}, bf16[2,48,384]{2,1,0:T(8,128)(2,1)S(1)}, u32[]{:S(2)}, u32[]{:S(2)}) collective-permute-start(bf16[2,48,384]{2,1,0:T(8,128)(2,1)S(1)} %get-tuple-element.14), channel_id=1, source_target_pairs={{0,72},{8,64},{64,136},{72,128},{128,200},{136,192},{192,8},{200,0... | collective-permute-start | bytes 221192 | tf_op jit(solution)/shard_map/ppermute | solution.py:302
  199.9 12.6 %collective-permute-start.6 = (bf16[2,48,384]{2,1,0:T(8,128)(2,1)S(1)}, bf16[2,48,384]{2,1,0:T(8,128)(2,1)S(1)}, u32[]{:S(2)}, u32[]{:S(2)}) collective-permute-start(bf16[2,48,384]{2,1,0:T(8,128)(2,1)S(1)} %get-tuple-element.14), channel_id=1, source_target_pairs={{0,128},{8,136},{64,192},{72,200},{128,0},{136,8},{192,64},{200,72... | collective-permute-start | bytes 221192 | tf_op jit(solution)/shard_map/ppermute | solution.py:302
  203.0 9.6 %collective-permute-start.7 = (bf16[2,48,384]{2,1,0:T(8,128)(2,1)S(1)}, bf16[2,48,384]{2,1,0:T(8,128)(2,1)S(1)}, u32[]{:S(2)}, u32[]{:S(2)}) collective-permute-start(bf16[2,48,384]{2,1,0:T(8,128)(2,1)S(1)} %get-tuple-element.14), channel_id=1, source_target_pairs={{0,136},{8,128},{64,200},{72,192},{128,8},{136,0},{192,72},{200,64... | collective-permute-start | bytes 221192 | tf_op jit(solution)/shard_map/ppermute | solution.py:302
  203.9 26.6 %all-to-all-start.2 = ((bf16[8,2,48,384]{3,2,1,0:T(8,128)(2,1)}), bf16[8,2,48,384]{3,2,1,0:T(8,128)(2,1)S(1)}, u32[]{:S(2)}, u32[]{:S(2)}) async-start(bf16[8,2,48,384]{3,2,1,0:T(8,128)(2,1)} %get-tuple-element.13), calls=%async_computation.2 | async-start | bytes 1179648 | tf_op jit(solution)/shard_map/all_to_all | solution.py:261
  208.2 7.2 %collective-permute-start.8 = (bf16[2,48,384]{2,1,0:T(8,128)(2,1)S(1)}, bf16[2,48,384]{2,1,0:T(8,128)(2,1)S(1)}, u32[]{:S(2)}, u32[]{:S(2)}) collective-permute-start(bf16[2,48,384]{2,1,0:T(8,128)(2,1)S(1)} %get-tuple-element.14), channel_id=1, source_target_pairs={{0,192},{8,200},{64,0},{72,8},{128,64},{136,72},{192,128},{200,136... | collective-permute-start | bytes 221192 | tf_op jit(solution)/shard_map/ppermute | solution.py:302
  210.9 4.8 %collective-permute-start.9 = (bf16[2,48,384]{2,1,0:T(8,128)(2,1)S(1)}, bf16[2,48,384]{2,1,0:T(8,128)(2,1)S(1)}, u32[]{:S(2)}, u32[]{:S(2)}) collective-permute-start(bf16[2,48,384]{2,1,0:T(8,128)(2,1)S(1)} %get-tuple-element.14), channel_id=1, source_target_pairs={{0,200},{8,192},{64,8},{72,0},{128,72},{136,64},{192,136},{200,128... | collective-permute-start | bytes 221192 | tf_op jit(solution)/shard_map/ppermute | solution.py:302
  215.8 7.2 %collective-permute-start.10 = (bf16[16,48,384]{2,1,0:T(8,128)(2,1)S(1)}, bf16[16,48,384]{2,1,0:T(8,128)(2,1)S(1)}, u32[]{:S(2)}, u32[]{:S(2)}) collective-permute-start(bf16[16,48,384]{2,1,0:T(8,128)(2,1)S(1)} %constant_dynamic-update-slice_fusion.own_ref), channel_id=1, source_target_pairs={{0,1},{1,0},{2,3},{3,2},{4,5},{5,4},{6,7},{7,6},{8,9},{9,8},{10,11... | collective-permute-start | bytes 1769480 | tf_op jit(solution)/shard_map/ppermute | solution.py:304
  223.0 2.8 copy-start.1
  230.5 34.5 %all-to-all-start.4 = ((bf16[128,24,128]{2,1,0:T(8,128)(2,1)}), bf16[128,24,128]{2,1,0:T(8,128)(2,1)S(1)}, u32[]{:S(2)}, u32[]{:S(2)}) async-start(bf16[128,24,128]{2,1,0:T(8,128)(2,1)} %bitcast.10), calls=%async_computation.4 | async-start | bytes 1572864 | tf_op jit(solution)/shard_map/all_to_all | solution.py:261
  240.0 2.4 collective-permute-start.2
  242.4 2.8 copy-start.2

commit v7 on v5

--- a/solution.py
+++ b/solution.py
@@ -228,10 +228,11 @@
     rows = BLOCK // 2
 
     def put(k, carry):
+        slot = k % (NZB * NZC) * NY + k // (NZB * NZC)
         for h in range(NX // 2):
             pair = halves(*[acc_ref[k, r * rows:(r + 1) * rows, h * LANE:(h + 1) * LANE] for r in range(2)])
             for t in range(2):
-                o_ref[2 * h + t, k] = pair[t].astype(o_ref.dtype)
+                o_ref[slot, 2 * h + t] = pair[t].astype(o_ref.dtype)
         return carry
 
     lax.fori_loop(0, CLUSTERS, put, 0, unroll=2)
@@ -243,7 +244,7 @@
         compiler_params=SMALL,
         in_specs=[SMEM, SMEM, SMEM, VMEM, VMEM, VMEM],
         out_specs=VMEM,
-        out_shape=jax.ShapeDtypeStruct((NX, CLUSTERS, BLOCK // 2, LANE), jnp.bfloat16),
+        out_shape=jax.ShapeDtypeStruct((CLUSTERS, NX, BLOCK // 2, LANE), jnp.bfloat16),
         scratch_shapes=[pltpu.VMEM((CLUSTERS, BLOCK, COLS), jnp.float32)],
     )(cluster_ids, weight, core, got, columns, sums)
 
@@ -259,7 +260,7 @@
             put(x - 2).wait()
         for zb in range(NZB):
             for y in range(NY):
-                pair = halves(m_ref[x, y, zb, 0], m_ref[x, y, zb, 1])
+                pair = halves(m_ref[zb, 0, y, x], m_ref[zb, 1, y, x])
                 buf_ref[x % 2, zb * BLOCK:(zb + 1) * BLOCK, y * LANE:(y + 1) * LANE] = jnp.concatenate(pair, 0)
         put(x).start()
     for x in range(NX - 2, NX):
@@ -307,14 +308,14 @@
 
     got = lax.ppermute(grams(anchor_of, core, columns, True), "core", SWAP)
     partial = ((grams(anchor_of, core, columns, False) + got) * SCALE).astype(jnp.float16)
-    parts = exchange(partial, ("y", "zc")).astype(jnp.float32)
+    parts = exchange(partial, ("zc", "y")).astype(jnp.float32)
     copies = polars(parts.reshape(SLICES, MINE, BLOCK, LANES))
-    own = exchange(copies, ("y", "zc")).reshape(GROUPS, BLOCK, LANES)
+    own = exchange(copies, ("zc", "y")).reshape(GROUPS, BLOCK, LANES)
     got = lax.ppermute(own, "core", SWAP)
     merged = align_got(cluster_ids, weight, core, got, columns, align_own(cluster_ids, weight, core, own, columns))
 
-    merged = exchange(merged.reshape(-1, BLOCK // 2, LANE), ("x", "y", "zb", "zc"))
-    return final(merged.reshape(NX, NY, NZB, NZC, BLOCK // 2, LANE))
+    merged = exchange(merged.reshape(-1, BLOCK // 2, LANE), ("zb", "zc", "y", "x"))
+    return final(merged.reshape(NZB, NZC, NY, NX, BLOCK // 2, LANE))
 
 
 def solution(mesh):

time: 276 us -> 275 us (level)
  blocking collectives: 238 us -> 235 us
    all_to_all x4, blocking collectives: 238 us -> 235 us  [exchange(): return lax.all_to_all(value, axes, split_axis=0, concat_axis=0, tiled=True)]
where the time goes in v7:
time: 275 us; the launch traced here: 274 us
  blocking collectives  235 us (85%)
  Pallas kernels  27.1 us (10%)
  starting transfers between devices  7.55 us (3%)
  waiting for transfers between devices  2.88 us (1%)
    all_to_all x4, blocking collectives, exchange(): return lax.all_to_all(value, axes, split_axis=0, concat_axis=0, tiled=True)  235 us
    pallas_call x3, Pallas kernels, spread(): pl.pallas_call(kernel, compiler_params=LARGE if other else MEDIUM, in_spe...  8.47 us
    pallas_call x1, Pallas kernels, polars(): pl.pallas_call(polar_kernel, compiler_params=SMALL, in_specs=[VMEM], out_...  6.04 us
  transfers between devices with their start and end apart: 4, of which 3 were waited for; matrix products, arithmetic and copies ran while one was open for 0% of the time, Pallas kernels for 4%

profile of v7, /device:TPU:1, one launch (start us, length us, event | category | flops | bytes accessed | tf_op | source)
XLA Modules:
  0.0 273.8 jit_solution(232770199733397148)
XLA Ops:
  0.0 2.9 %shard_map.37 = bf16[2,8,2,96,256]{4,3,2,1,0:T(8,128)(2,1)} custom-call(s32[1]{0:T(128)} %bitcast.1.core_ref, bf16[4,192,4096]{2,1,0:T(8,128)(2,1)} %w_ref.5), custom_call_target="tpu_custom_call" | custom-call | tf_op jit(solution)/shard_map/pallas_call | solution.py:75
  3.0 3.3 %collective-permute-start = (bf16[2,8,2,96,256]{4,3,2,1,0:T(8,128)(2,1)}, bf16[2,8,2,96,256]{4,3,2,1,0:T(8,128)(2,1)S(1)}, u32[]{:S(2)}, u32[]{:S(2)}) collective-permute-start(bf16[2,8,2,96,256]{4,3,2,1,0:T(8,128)(2,1)} %shard_map.37), channel_id=1, source_target_pairs={{0,1},{1,0},{2,3},{3,2},{4,5},{5,4},{6,7},{7,6},{8,9},{9,8},{10,11... | collective-permute-start | bytes 4718600 | tf_op jit(solution)/shard_map/ppermute | solution.py:303
  6.2 3.0 %shard_map.38 = bf16[2,8,2,96,256]{4,3,2,1,0:T(8,128)(2,1)} custom-call(s32[1]{0:T(128)} %bitcast.1.core_ref, bf16[4,192,4096]{2,1,0:T(8,128)(2,1)} %w_ref.5), custom_call_target="tpu_custom_call" | custom-call | tf_op jit(solution)/shard_map/pallas_call | solution.py:75
  9.3 2.6 shard_map.39.refs_2_
  11.9 0.1 select_reduce_fusion.3
  12.1 0.1 select_reduce_fusion.1
  12.3 0.6 collective-permute-done.1.refs_1_
  12.9 0.2 shard_map.40
  13.2 148.8 %all_to_all.20 = bf16[32,384,256]{2,1,0:T(8,128)(2,1)S(1)} all-to-all(bf16[32,384,256]{2,1,0:T(8,128)(2,1)S(1)} %bitcast.13), channel_id=1, replica_groups=mesh['y'=4,'zb'=4,'zc'=2,'x'=4,'core'=2] {'zb','y','zc'}, dimensions={0} | all-to-all | bytes 12582912 | tf_op jit(solution)/shard_map/all_to_all | solution.py:284
  161.9 2.3 shard_map.42
  164.2 1.2 collective-permute-start.2
  165.4 2.3 shard_map.41
  167.7 1.9 collective-permute-done.2
  169.6 0.4 multiply_convert_fusion
  170.0 21.1 %all_to_all.21 = f16[16,96,384]{2,1,0:T(8,128)(2,1)S(1)} all-to-all(f16[16,96,384]{2,1,0:T(8,128)(2,1)S(1)} %multiply_convert_fusion), channel_id=1, replica_groups=mesh['y'=4,'zb'=4,'zc'=2,'x'=4,'core'=2] {'zc','y'}, dimensions={0} | all-to-all | bytes 2359296 | tf_op jit(solution)/shard_map/all_to_all | solution.py:284
  191.1 0.2 convert.1.part_ref
  191.3 6.0 %shard_map.43 = bf16[8,2,96,384]{3,2,1,0:T(8,128)(2,1)S(1)} custom-call(f32[8,2,96,384]{3,2,1,0:T(8,128)S(1)} %convert.1.part_ref), custom_call_target="tpu_custom_call" | custom-call | tf_op jit(solution)/shard_map/pallas_call | solution.py:184
  197.4 18.1 %all_to_all.22 = bf16[8,2,96,384]{3,2,1,0:T(8,128)(2,1)S(1)} all-to-all(bf16[8,2,96,384]{3,2,1,0:T(8,128)(2,1)S(1)} %shard_map.43), channel_id=1, replica_groups=mesh['y'=4,'zb'=4,'zc'=2,'x'=4,'core'=2] {'zc','y'}, dimensions={0} | all-to-all | bytes 2359296 | tf_op jit(solution)/shard_map/all_to_all | solution.py:284
  215.4 2.9 %collective-permute-start.3 = (bf16[16,96,384]{2,1,0:T(8,128)(2,1)S(1)}, bf16[16,96,384]{2,1,0:T(8,128)(2,1)S(1)}, u32[]{:S(2)}, u32[]{:S(2)}) collective-permute-start(bf16[16,96,384]{2,1,0:T(8,128)(2,1)S(1)} %bitcast.16), channel_id=1, source_target_pairs={{0,1},{1,0},{2,3},{3,2},{4,5},{5,4},{6,7},{7,6},{8,9},{9,8},{10,11... | collective-permute-start | bytes 3538952 | tf_op jit(solution)/shard_map/ppermute | solution.py:314
  218.4 2.1 shard_map.44.sum_ref
  220.5 0.3 collective-permute-done.3.got_ref
  220.9 3.7 %shard_map.45 = bf16[32,4,48,128]{3,2,1,0:T(8,128)(2,1)S(1)} custom-call(s32[128]{0:T(128)S(1)} %bitcast.22, f32[128]{0:T(128)S(1)} %convert_divide_fusion.weight_ref, s32[1]{0:T(128)} %bitcast.1.core_ref, bf16[16,96,384]{2,1,0:T(8,128)(2,1)S(1)} %collective-permute-done.3.got_ref, bf16[128,96,256]{2,1,0:T(8,128)(2,1)S(1)} %bitcast.12, ...), custom_call_target="tpu_custom_call" | custom-call | tf_op jit(solution)/shard_map/pallas_call | solution.py:242
  224.6 47.3 %all_to_all.23 = bf16[128,48,128]{2,1,0:T(8,128)(2,1)S(1)} all-to-all(bf16[128,48,128]{2,1,0:T(8,128)(2,1)S(1)} %bitcast.14), channel_id=1, replica_groups=mesh['y'=4,'zb'=4,'zc'=2,'x'=4,'core'=2] {'zb','zc','y','x'}, dimensions={0} | all-to-all | bytes 3145728 | tf_op jit(solution)/shard_map/all_to_all | solution.py:284
  271.8 2.0 shard_map.46
  (11 shorter events, 0.2 us)
Async XLA Ops:
  3.0 9.3 %collective-permute-start = (bf16[2,8,2,96,256]{4,3,2,1,0:T(8,128)(2,1)}, bf16[2,8,2,96,256]{4,3,2,1,0:T(8,128)(2,1)S(1)}, u32[]{:S(2)}, u32[]{:S(2)}) collective-permute-start(bf16[2,8,2,96,256]{4,3,2,1,0:T(8,128)(2,1)} %shard_map.37), channel_id=1, source_target_pairs={{0,1},{1,0},{2,3},{3,2},{4,5},{5,4},{6,7},{7,6},{8,9},{9,8},{10,11... | collective-permute-start | bytes 4718600 | tf_op jit(solution)/shard_map/ppermute | solution.py:303
  9.2 2.7 copy-start.1
  9.2 2.7 copy-start
  9.2 3.7 %collective-permute-start.1 = (bf16[2,8,2,96,256]{4,3,2,1,0:T(8,128)(2,1)}, bf16[2,8,2,96,256]{4,3,2,1,0:T(8,128)(2,1)S(1)}, u32[]{:S(2)}, u32[]{:S(2)}) collective-permute-start(bf16[2,8,2,96,256]{4,3,2,1,0:T(8,128)(2,1)} %shard_map.38), channel_id=1, source_target_pairs={{0,1},{1,0},{2,3},{3,2},{4,5},{5,4},{6,7},{7,6},{8,9},{9,8},{10,11... | collective-permute-start | bytes 4718600 | tf_op jit(solution)/shard_map/ppermute | solution.py:303
  164.2 5.4 %collective-permute-start.2 = (f32[16,96,384]{2,1,0:T(8,128)S(1)}, f32[16,96,384]{2,1,0:T(8,128)S(1)}, u32[]{:S(2)}, u32[]{:S(2)}) collective-permute-start(f32[16,96,384]{2,1,0:T(8,128)S(1)} %shard_map.42), channel_id=1, source_target_pairs={{0,1},{1,0},{2,3},{3,2},{4,5},{5,4},{6,7},{7,6},{8,9},{9,8},{10,11... | collective-permute-start | bytes 7077896 | tf_op jit(solution)/shard_map/ppermute | solution.py:309
  215.4 5.4 %collective-permute-start.3 = (bf16[16,96,384]{2,1,0:T(8,128)(2,1)S(1)}, bf16[16,96,384]{2,1,0:T(8,128)(2,1)S(1)}, u32[]{:S(2)}, u32[]{:S(2)}) collective-permute-start(bf16[16,96,384]{2,1,0:T(8,128)(2,1)S(1)} %bitcast.16), channel_id=1, source_target_pairs={{0,1},{1,0},{2,3},{3,2},{4,5},{5,4},{6,7},{7,6},{8,9},{9,8},{10,11... | collective-permute-start | bytes 3538952 | tf_op jit(solution)/shard_map/ppermute | solution.py:314

commit v8 on v7

--- a/solution.py
+++ b/solution.py
@@ -306,8 +306,9 @@
     rows, anchor_of, weight = lax.optimization_barrier((rows, anchor_of, weight))
     columns = exchange(rows, ("zb", "y", "zc")).reshape(EXPERTS, BLOCK, COLS)
 
-    got = lax.ppermute(grams(anchor_of, core, columns, True), "core", SWAP)
-    partial = ((grams(anchor_of, core, columns, False) + got) * SCALE).astype(jnp.float16)
+    send = (grams(anchor_of, core, columns, True) * SCALE).astype(jnp.float16)
+    got = lax.ppermute(send, "core", SWAP).astype(jnp.float32)
+    partial = (grams(anchor_of, core, columns, False) * SCALE + got).astype(jnp.float16)
     parts = exchange(partial, ("zc", "y")).astype(jnp.float32)
     copies = polars(parts.reshape(SLICES, MINE, BLOCK, LANES))
     own = exchange(copies, ("zc", "y")).reshape(GROUPS, BLOCK, LANES)

time: 275 us -> 274 us (level)
  no operation moved by 1% of the time
where the time goes in v8:
time: 274 us; the launch traced here: 272 us
  blocking collectives  235 us (86%)
  Pallas kernels  27 us (10%)
  starting transfers between devices  7.55 us (3%)
    all_to_all x4, blocking collectives, exchange(): return lax.all_to_all(value, axes, split_axis=0, concat_axis=0, tiled=True)  235 us
    pallas_call x3, Pallas kernels, spread(): pl.pallas_call(kernel, compiler_params=LARGE if other else MEDIUM, in_spe...  8.47 us
    pallas_call x1, Pallas kernels, polars(): pl.pallas_call(polar_kernel, compiler_params=SMALL, in_specs=[VMEM], out_...  6.04 us
  transfers between devices with their start and end apart: 4, of which 3 were waited for; matrix products, arithmetic and copies ran while one was open for 0% of the time, Pallas kernels for 4%

profile of v8, /device:TPU:1, one launch (start us, length us, event | category | flops | bytes accessed | tf_op | source)
XLA Modules:
  0.0 272.3 jit_solution(2741991111918873222)
XLA Ops:
  0.0 2.9 %shard_map.37 = bf16[2,8,2,96,256]{4,3,2,1,0:T(8,128)(2,1)} custom-call(s32[1]{0:T(128)} %bitcast.1.core_ref, bf16[4,192,4096]{2,1,0:T(8,128)(2,1)} %w_ref.5), custom_call_target="tpu_custom_call" | custom-call | tf_op jit(solution)/shard_map/pallas_call | solution.py:75
  3.0 3.3 %collective-permute-start = (bf16[2,8,2,96,256]{4,3,2,1,0:T(8,128)(2,1)}, bf16[2,8,2,96,256]{4,3,2,1,0:T(8,128)(2,1)S(1)}, u32[]{:S(2)}, u32[]{:S(2)}) collective-permute-start(bf16[2,8,2,96,256]{4,3,2,1,0:T(8,128)(2,1)} %shard_map.37), channel_id=1, source_target_pairs={{0,1},{1,0},{2,3},{3,2},{4,5},{5,4},{6,7},{7,6},{8,9},{9,8},{10,11... | collective-permute-start | bytes 4718600 | tf_op jit(solution)/shard_map/ppermute | solution.py:303
  6.2 3.0 %shard_map.38 = bf16[2,8,2,96,256]{4,3,2,1,0:T(8,128)(2,1)} custom-call(s32[1]{0:T(128)} %bitcast.1.core_ref, bf16[4,192,4096]{2,1,0:T(8,128)(2,1)} %w_ref.5), custom_call_target="tpu_custom_call" | custom-call | tf_op jit(solution)/shard_map/pallas_call | solution.py:75
  9.3 2.6 shard_map.39.refs_2_
  12.1 0.1 select_reduce_fusion.1
  12.3 0.6 collective-permute-done.1.refs_1_
  12.9 0.2 shard_map.40
  13.2 148.8 %all_to_all.20 = bf16[32,384,256]{2,1,0:T(8,128)(2,1)S(1)} all-to-all(bf16[32,384,256]{2,1,0:T(8,128)(2,1)S(1)} %bitcast.13), channel_id=1, replica_groups=mesh['y'=4,'zb'=4,'zc'=2,'x'=4,'core'=2] {'zb','y','zc'}, dimensions={0} | all-to-all | bytes 12582912 | tf_op jit(solution)/shard_map/all_to_all | solution.py:284
  161.9 2.3 shard_map.42
  164.2 0.3 multiply_convert_fusion
  164.5 1.2 collective-permute-start.2
  165.7 2.3 shard_map.41
  168.0 0.2 collective-permute-done.2
  168.2 0.4 add_convert_fusion
  168.5 21.1 %all_to_all.21 = f16[16,96,384]{2,1,0:T(8,128)(2,1)S(1)} all-to-all(f16[16,96,384]{2,1,0:T(8,128)(2,1)S(1)} %add_convert_fusion), channel_id=1, replica_groups=mesh['y'=4,'zb'=4,'zc'=2,'x'=4,'core'=2] {'zc','y'}, dimensions={0} | all-to-all | bytes 2359296 | tf_op jit(solution)/shard_map/all_to_all | solution.py:284
  189.6 0.2 convert.1.part_ref
  189.9 6.0 %shard_map.43 = bf16[8,2,96,384]{3,2,1,0:T(8,128)(2,1)S(1)} custom-call(f32[8,2,96,384]{3,2,1,0:T(8,128)S(1)} %convert.1.part_ref), custom_call_target="tpu_custom_call" | custom-call | tf_op jit(solution)/shard_map/pallas_call | solution.py:184
  195.9 18.1 %all_to_all.22 = bf16[8,2,96,384]{3,2,1,0:T(8,128)(2,1)S(1)} all-to-all(bf16[8,2,96,384]{3,2,1,0:T(8,128)(2,1)S(1)} %shard_map.43), channel_id=1, replica_groups=mesh['y'=4,'zb'=4,'zc'=2,'x'=4,'core'=2] {'zc','y'}, dimensions={0} | all-to-all | bytes 2359296 | tf_op jit(solution)/shard_map/all_to_all | solution.py:284
  214.0 2.9 %collective-permute-start.3 = (bf16[16,96,384]{2,1,0:T(8,128)(2,1)S(1)}, bf16[16,96,384]{2,1,0:T(8,128)(2,1)S(1)}, u32[]{:S(2)}, u32[]{:S(2)}) collective-permute-start(bf16[16,96,384]{2,1,0:T(8,128)(2,1)S(1)} %bitcast.16), channel_id=1, source_target_pairs={{0,1},{1,0},{2,3},{3,2},{4,5},{5,4},{6,7},{7,6},{8,9},{9,8},{10,11... | collective-permute-start | bytes 3538952 | tf_op jit(solution)/shard_map/ppermute | solution.py:315
  216.9 2.1 shard_map.44.sum_ref
  219.0 0.4 collective-permute-done.3.got_ref
  219.4 3.6 %shard_map.45 = bf16[32,4,48,128]{3,2,1,0:T(8,128)(2,1)S(1)} custom-call(s32[128]{0:T(128)S(1)} %bitcast.22, f32[128]{0:T(128)S(1)} %convert_divide_fusion.weight_ref, s32[1]{0:T(128)} %bitcast.1.core_ref, bf16[16,96,384]{2,1,0:T(8,128)(2,1)S(1)} %collective-permute-done.3.got_ref, bf16[128,96,256]{2,1,0:T(8,128)(2,1)S(1)} %bitcast.12, ...), custom_call_target="tpu_custom_call" | custom-call | tf_op jit(solution)/shard_map/pallas_call | solution.py:242
  223.0 47.2 %all_to_all.23 = bf16[128,48,128]{2,1,0:T(8,128)(2,1)S(1)} all-to-all(bf16[128,48,128]{2,1,0:T(8,128)(2,1)S(1)} %bitcast.14), channel_id=1, replica_groups=mesh['y'=4,'zb'=4,'zc'=2,'x'=4,'core'=2] {'zb','zc','y','x'}, dimensions={0} | all-to-all | bytes 3145728 | tf_op jit(solution)/shard_map/all_to_all | solution.py:284
  270.3 2.0 shard_map.46
  (12 shorter events, 0.4 us)
Async XLA Ops:
  3.0 9.3 %collective-permute-start = (bf16[2,8,2,96,256]{4,3,2,1,0:T(8,128)(2,1)}, bf16[2,8,2,96,256]{4,3,2,1,0:T(8,128)(2,1)S(1)}, u32[]{:S(2)}, u32[]{:S(2)}) collective-permute-start(bf16[2,8,2,96,256]{4,3,2,1,0:T(8,128)(2,1)} %shard_map.37), channel_id=1, source_target_pairs={{0,1},{1,0},{2,3},{3,2},{4,5},{5,4},{6,7},{7,6},{8,9},{9,8},{10,11... | collective-permute-start | bytes 4718600 | tf_op jit(solution)/shard_map/ppermute | solution.py:303
  9.2 2.7 copy-start.1
  9.2 2.7 copy-start
  9.2 3.7 %collective-permute-start.1 = (bf16[2,8,2,96,256]{4,3,2,1,0:T(8,128)(2,1)}, bf16[2,8,2,96,256]{4,3,2,1,0:T(8,128)(2,1)S(1)}, u32[]{:S(2)}, u32[]{:S(2)}) collective-permute-start(bf16[2,8,2,96,256]{4,3,2,1,0:T(8,128)(2,1)} %shard_map.38), channel_id=1, source_target_pairs={{0,1},{1,0},{2,3},{3,2},{4,5},{5,4},{6,7},{7,6},{8,9},{9,8},{10,11... | collective-permute-start | bytes 4718600 | tf_op jit(solution)/shard_map/ppermute | solution.py:303
  164.5 3.7 %collective-permute-start.2 = (f16[16,96,384]{2,1,0:T(8,128)(2,1)S(1)}, f16[16,96,384]{2,1,0:T(8,128)(2,1)S(1)}, u32[]{:S(2)}, u32[]{:S(2)}) collective-permute-start(f16[16,96,384]{2,1,0:T(8,128)(2,1)S(1)} %multiply_convert_fusion), channel_id=1, source_target_pairs={{0,1},{1,0},{2,3},{3,2},{4,5},{5,4},{6,7},{7,6},{8,9},{9,8},{10,11... | collective-permute-start | bytes 3538952 | tf_op jit(solution)/shard_map/ppermute | solution.py:310
  214.0 5.4 %collective-permute-start.3 = (bf16[16,96,384]{2,1,0:T(8,128)(2,1)S(1)}, bf16[16,96,384]{2,1,0:T(8,128)(2,1)S(1)}, u32[]{:S(2)}, u32[]{:S(2)}) collective-permute-start(bf16[16,96,384]{2,1,0:T(8,128)(2,1)S(1)} %bitcast.16), channel_id=1, source_target_pairs={{0,1},{1,0},{2,3},{3,2},{4,5},{5,4},{6,7},{7,6},{8,9},{9,8},{10,11... | collective-permute-start | bytes 3538952 | tf_op jit(solution)/shard_map/ppermute | solution.py:315

commit v9 on v8

--- a/solution.py
+++ b/solution.py
@@ -120,7 +120,7 @@
             o_ref[g] = jnp.concatenate(parts, axis=1)
             return carry
 
-        lax.fori_loop(0, GROUPS, step, 0, unroll=4)
+        lax.fori_loop(0, GROUPS, step, 0, unroll=8)
 
     return pl.pallas_call(
         kernel,

time: 274 us -> 273 us (level)
  transfers between devices with their start and end apart: 4 -> 4, of which waited for: 3 -> 3; matrix products, arithmetic and copies ran while one was open for 0% -> 0% of each run, Pallas kernels for 4% -> 3%
where the time goes in v9:
time: 273 us; the launch traced here: 272 us
  blocking collectives  235 us (86%)
  Pallas kernels  26.1 us (10%)
  starting transfers between devices  7.55 us (3%)
    all_to_all x4, blocking collectives, exchange(): return lax.all_to_all(value, axes, split_axis=0, concat_axis=0, tiled=True)  235 us
    pallas_call x3, Pallas kernels, spread(): pl.pallas_call(kernel, compiler_params=LARGE if other else MEDIUM, in_spe...  8.47 us
    pallas_call x1, Pallas kernels, polars(): pl.pallas_call(polar_kernel, compiler_params=SMALL, in_specs=[VMEM], out_...  6.05 us
  transfers between devices with their start and end apart: 4, of which 3 were waited for; matrix products, arithmetic and copies ran while one was open for 0% of the time, Pallas kernels for 3%

profile of v9, /device:TPU:1, one launch (start us, length us, event | category | flops | bytes accessed | tf_op | source)
XLA Modules:
  0.0 271.8 jit_solution(11406314216502959211)
XLA Ops:
  0.0 2.9 %shard_map.37 = bf16[2,8,2,96,256]{4,3,2,1,0:T(8,128)(2,1)} custom-call(s32[1]{0:T(128)} %bitcast.1.core_ref, bf16[4,192,4096]{2,1,0:T(8,128)(2,1)} %w_ref.5), custom_call_target="tpu_custom_call" | custom-call | tf_op jit(solution)/shard_map/pallas_call | solution.py:75
  3.0 3.3 %collective-permute-start = (bf16[2,8,2,96,256]{4,3,2,1,0:T(8,128)(2,1)}, bf16[2,8,2,96,256]{4,3,2,1,0:T(8,128)(2,1)S(1)}, u32[]{:S(2)}, u32[]{:S(2)}) collective-permute-start(bf16[2,8,2,96,256]{4,3,2,1,0:T(8,128)(2,1)} %shard_map.37), channel_id=1, source_target_pairs={{0,1},{1,0},{2,3},{3,2},{4,5},{5,4},{6,7},{7,6},{8,9},{9,8},{10,11... | collective-permute-start | bytes 4718600 | tf_op jit(solution)/shard_map/ppermute | solution.py:303
  6.2 3.0 %shard_map.38 = bf16[2,8,2,96,256]{4,3,2,1,0:T(8,128)(2,1)} custom-call(s32[1]{0:T(128)} %bitcast.1.core_ref, bf16[4,192,4096]{2,1,0:T(8,128)(2,1)} %w_ref.5), custom_call_target="tpu_custom_call" | custom-call | tf_op jit(solution)/shard_map/pallas_call | solution.py:75
  9.3 2.6 shard_map.39.refs_2_
  12.1 0.1 select_reduce_fusion.1
  12.3 0.6 collective-permute-done.1.refs_1_
  12.9 0.2 shard_map.40
  13.2 148.8 %all_to_all.20 = bf16[32,384,256]{2,1,0:T(8,128)(2,1)S(1)} all-to-all(bf16[32,384,256]{2,1,0:T(8,128)(2,1)S(1)} %bitcast.13), channel_id=1, replica_groups=mesh['y'=4,'zb'=4,'zc'=2,'x'=4,'core'=2] {'zb','y','zc'}, dimensions={0} | all-to-all | bytes 12582912 | tf_op jit(solution)/shard_map/all_to_all | solution.py:284
  161.9 1.8 shard_map.42
  163.8 0.3 multiply_convert_fusion
  164.0 1.2 collective-permute-start.2
  165.2 1.8 shard_map.41
  167.1 0.7 collective-permute-done.2
  167.7 0.4 add_convert_fusion
  168.1 21.1 %all_to_all.21 = f16[16,96,384]{2,1,0:T(8,128)(2,1)S(1)} all-to-all(f16[16,96,384]{2,1,0:T(8,128)(2,1)S(1)} %add_convert_fusion), channel_id=1, replica_groups=mesh['y'=4,'zb'=4,'zc'=2,'x'=4,'core'=2] {'zc','y'}, dimensions={0} | all-to-all | bytes 2359296 | tf_op jit(solution)/shard_map/all_to_all | solution.py:284
  189.2 0.2 convert.1.part_ref
  189.4 6.0 %shard_map.43 = bf16[8,2,96,384]{3,2,1,0:T(8,128)(2,1)S(1)} custom-call(f32[8,2,96,384]{3,2,1,0:T(8,128)S(1)} %convert.1.part_ref), custom_call_target="tpu_custom_call" | custom-call | tf_op jit(solution)/shard_map/pallas_call | solution.py:184
  195.5 18.1 %all_to_all.22 = bf16[8,2,96,384]{3,2,1,0:T(8,128)(2,1)S(1)} all-to-all(bf16[8,2,96,384]{3,2,1,0:T(8,128)(2,1)S(1)} %shard_map.43), channel_id=1, replica_groups=mesh['y'=4,'zb'=4,'zc'=2,'x'=4,'core'=2] {'zc','y'}, dimensions={0} | all-to-all | bytes 2359296 | tf_op jit(solution)/shard_map/all_to_all | solution.py:284
  213.5 2.9 %collective-permute-start.3 = (bf16[16,96,384]{2,1,0:T(8,128)(2,1)S(1)}, bf16[16,96,384]{2,1,0:T(8,128)(2,1)S(1)}, u32[]{:S(2)}, u32[]{:S(2)}) collective-permute-start(bf16[16,96,384]{2,1,0:T(8,128)(2,1)S(1)} %bitcast.16), channel_id=1, source_target_pairs={{0,1},{1,0},{2,3},{3,2},{4,5},{5,4},{6,7},{7,6},{8,9},{9,8},{10,11... | collective-permute-start | bytes 3538952 | tf_op jit(solution)/shard_map/ppermute | solution.py:315
  216.5 2.1 shard_map.44.sum_ref
  218.6 0.4 collective-permute-done.3.got_ref
  219.0 3.6 %shard_map.45 = bf16[32,4,48,128]{3,2,1,0:T(8,128)(2,1)S(1)} custom-call(s32[128]{0:T(128)S(1)} %bitcast.22, f32[128]{0:T(128)S(1)} %convert_divide_fusion.weight_ref, s32[1]{0:T(128)} %bitcast.1.core_ref, bf16[16,96,384]{2,1,0:T(8,128)(2,1)S(1)} %collective-permute-done.3.got_ref, bf16[128,96,256]{2,1,0:T(8,128)(2,1)S(1)} %bitcast.12, ...), custom_call_target="tpu_custom_call" | custom-call | tf_op jit(solution)/shard_map/pallas_call | solution.py:242
  222.6 47.2 %all_to_all.23 = bf16[128,48,128]{2,1,0:T(8,128)(2,1)S(1)} all-to-all(bf16[128,48,128]{2,1,0:T(8,128)(2,1)S(1)} %bitcast.14), channel_id=1, replica_groups=mesh['y'=4,'zb'=4,'zc'=2,'x'=4,'core'=2] {'zb','zc','y','x'}, dimensions={0} | all-to-all | bytes 3145728 | tf_op jit(solution)/shard_map/all_to_all | solution.py:284
  269.8 2.0 shard_map.46
  (12 shorter events, 0.4 us)
Async XLA Ops:
  3.0 9.3 %collective-permute-start = (bf16[2,8,2,96,256]{4,3,2,1,0:T(8,128)(2,1)}, bf16[2,8,2,96,256]{4,3,2,1,0:T(8,128)(2,1)S(1)}, u32[]{:S(2)}, u32[]{:S(2)}) collective-permute-start(bf16[2,8,2,96,256]{4,3,2,1,0:T(8,128)(2,1)} %shard_map.37), channel_id=1, source_target_pairs={{0,1},{1,0},{2,3},{3,2},{4,5},{5,4},{6,7},{7,6},{8,9},{9,8},{10,11... | collective-permute-start | bytes 4718600 | tf_op jit(solution)/shard_map/ppermute | solution.py:303
  9.2 2.7 copy-start.1
  9.2 2.7 copy-start
  9.2 3.7 %collective-permute-start.1 = (bf16[2,8,2,96,256]{4,3,2,1,0:T(8,128)(2,1)}, bf16[2,8,2,96,256]{4,3,2,1,0:T(8,128)(2,1)S(1)}, u32[]{:S(2)}, u32[]{:S(2)}) collective-permute-start(bf16[2,8,2,96,256]{4,3,2,1,0:T(8,128)(2,1)} %shard_map.38), channel_id=1, source_target_pairs={{0,1},{1,0},{2,3},{3,2},{4,5},{5,4},{6,7},{7,6},{8,9},{9,8},{10,11... | collective-permute-start | bytes 4718600 | tf_op jit(solution)/shard_map/ppermute | solution.py:303
  164.0 3.7 %collective-permute-start.2 = (f16[16,96,384]{2,1,0:T(8,128)(2,1)S(1)}, f16[16,96,384]{2,1,0:T(8,128)(2,1)S(1)}, u32[]{:S(2)}, u32[]{:S(2)}) collective-permute-start(f16[16,96,384]{2,1,0:T(8,128)(2,1)S(1)} %multiply_convert_fusion), channel_id=1, source_target_pairs={{0,1},{1,0},{2,3},{3,2},{4,5},{5,4},{6,7},{7,6},{8,9},{9,8},{10,11... | collective-permute-start | bytes 3538952 | tf_op jit(solution)/shard_map/ppermute | solution.py:310
  213.5 5.4 %collective-permute-start.3 = (bf16[16,96,384]{2,1,0:T(8,128)(2,1)S(1)}, bf16[16,96,384]{2,1,0:T(8,128)(2,1)S(1)}, u32[]{:S(2)}, u32[]{:S(2)}) collective-permute-start(bf16[16,96,384]{2,1,0:T(8,128)(2,1)S(1)} %bitcast.16), channel_id=1, source_target_pairs={{0,1},{1,0},{2,3},{3,2},{4,5},{5,4},{6,7},{7,6},{8,9},{9,8},{10,11... | collective-permute-start | bytes 3538952 | tf_op jit(solution)/shard_map/ppermute | solution.py:315
